TPU v7x, 32 devices: a whole 2x2x4 slice. The times are simulated.
32 devices in a mesh: lon: 2 (over x), lat: 4 (over z), lev: 4 (over y, core).
Axes of the slice: x: 2, y: 2, z: 4, core: 2. Of those that a mesh axis runs over, the one named last changes fastest.
Arguments:
- adjoint_in: float32 [8, 16, 16, 512], P(None, 'lev', 'lat', 'lon'), may hold values from -6 to 6
- courant_lon: float32 [16, 16, 512], P('lev', 'lat', 'lon'), may hold values from 0.05 to 0.45
- courant_lat: float32 [16, 16, 512], P('lev', 'lat', 'lon'), may hold values from 0.05 to 0.25
- horiz_diff: float32 [8], replicated, may hold values from 0.01 to 0.06
- vert_diff: float32 [16], replicated, may hold values from 0.01 to 0.1
- innovations: bfloat16 [512, 8, 16, 128], P(('lon', 'lat'), None, 'lev'), may hold values from -6 to 6
- obs_operator: bfloat16 [512, 128, 256], P(('lon', 'lat')), may hold values from -0.5 to 0.5
- owner_tile: int32 [512, 1], P(('lon', 'lat')), may hold values from 0 to 1; in each aligned block of 64 rows (0 to 63, 64 to 127, ...) at most 64 rows name the same one
- block_row: int32 [512], P(('lon', 'lat')), may hold values from 0 to 3
- obs_count: int32 [512], P(('lon', 'lat')), may hold values from 1 to 128
Outputs:
- adjoint_out: float32 [8, 16, 16, 512], P(None, 'lev', 'lat', 'lon')
Inputs may be any that keep to these rules, and one draw needn't show every extreme that they name: `owner_tile`: among the 64 blocks of one device at most 64 name the same longitude tile; in some device exactly 64 do.
All inputs are finite; a program needn't handle non-finite values.
Results may differ from a plain program's by a relative error of at most 0.002.
The roundings to bfloat16 on the way count: a program that leaves them out, or rounds other values in their place, can miss the bound.
Values may be sent and summed in bfloat16 or wider, within the bound.
No kernel may reach another device: no remote copies, remote signals or barrier semaphores. Data moves between devices by JAX's collectives and lax.ppermute only.
A program may use at most 64 MiB of HBM per device.

v0:
```python
import jax
import jax.numpy as jnp
from jax import lax
from jax.sharding import PartitionSpec as P

STEPS = 3


def extended_2(block, sides, width, periodic):
    for axis, dim in sides:
        count = lax.axis_size(axis)
        forward = [(i, i + 1) for i in range(count - 1)]
        if periodic:
            forward.append((count - 1, 0))
        backward = [(target, source) for source, target in forward]
        low = lax.ppermute(
            lax.slice_in_dim(block, block.shape[dim] - width, None, axis=dim), axis, forward
        )
        high = lax.ppermute(lax.slice_in_dim(block, 0, width, axis=dim), axis, backward)
        block = jnp.concatenate([low, block, high], axis=dim)
    return block


def widen(field, rim_width):
    beside_all = extended_2(field, (("lon", 3),), rim_width, True)
    return extended_2(beside_all, (("lat", 2), ("lev", 1)), rim_width, False)


def sweep(
    extended,
    wind_pair,
    horiz_diff,
    vert_diff,
    rim_width,
    lev_first,
    lat_first,
    level_total,
    lat_total,
):
    out_rim = rim_width - 1
    lev_glob = lev_first - out_rim + jnp.arange(extended.shape[1] - 2, dtype=jnp.int32)
    lat_glob = lat_first - out_rim + jnp.arange(extended.shape[2] - 2, dtype=jnp.int32)
    level_ids = jnp.arange(level_total, dtype=jnp.int32)
    coef_up = jnp.sum(
        jnp.where(
            (lev_glob[:, None] == level_ids[None, :]) & (level_ids[None, :] < level_total - 1),
            vert_diff[None, :],
            0.0,
        ),
        axis=1,
    )
    coef_down = jnp.sum(
        jnp.where(lev_glob[:, None] - 1 == level_ids[None, :], vert_diff[None, :], 0.0), axis=1
    )
    inside = (
        ((lev_glob >= 0) & (lev_glob < level_total))[:, None]
        & ((lat_glob >= 0) & (lat_glob < lat_total))[None, :]
    ).astype(jnp.float32)
    east_flux = wind_pair[0][None] * extended
    north_flux = wind_pair[1][None] * extended
    centre = extended[:, 1:-1, 1:-1, 1:-1]
    result = centre - east_flux[:, 1:-1, 1:-1, 1:-1] - north_flux[:, 1:-1, 1:-1, 1:-1]
    result = result + east_flux[:, 1:-1, 1:-1, 2:] + north_flux[:, 1:-1, 2:, 1:-1]
    spread = (
        extended[:, 1:-1, 1:-1, 2:]
        + extended[:, 1:-1, 1:-1, :-2]
        + extended[:, 1:-1, 2:, 1:-1]
        + extended[:, 1:-1, :-2, 1:-1]
        - 4.0 * centre
    )
    result = result + horiz_diff[:, None, None, None] * spread
    result = result + coef_up[None, :, None, None] * (extended[:, 2:, 1:-1, 1:-1] - centre)
    result = result + coef_down[None, :, None, None] * (extended[:, :-2, 1:-1, 1:-1] - centre)
    return result * inside[None, :, :, None]


def on_device(
    adjoint_in,
    courant_lon,
    courant_lat,
    horiz_diff,
    vert_diff,
    innovations,
    obs_operator,
    owner_tile,
    block_row,
    obs_count,
):
    num_fields = adjoint_in.shape[0]
    lev_cells = adjoint_in.shape[1]
    lat_cells = adjoint_in.shape[2]
    lon_cells = adjoint_in.shape[3]
    num_blocks = innovations.shape[0]
    obs_rows = innovations.shape[3]
    level_total = lev_cells * lax.axis_size("lev")
    lat_total = lat_cells * lax.axis_size("lat")
    lev_first = lax.axis_index("lev") * lev_cells
    lat_first = lax.axis_index("lat") * lat_cells
    observed = jnp.arange(obs_rows, dtype=jnp.int32)[None, :] < obs_count[:, None]
    masked = jnp.where(observed[:, None, None, :], innovations, jnp.zeros((), jnp.bfloat16))
    masked = masked.reshape(num_blocks, num_fields * lev_cells, obs_rows)
    products = jnp.einsum(
        "bvo,boc->bvc", masked, obs_operator, preferred_element_type=jnp.float32
    ).astype(jnp.bfloat16)
    flattened = products.reshape(num_blocks, num_fields * lev_cells * lon_cells)
    dest_tile = owner_tile[:, 0]
    target = dest_tile * lat_cells + block_row
    picks = (
        jnp.arange(lax.axis_size("lon") * lat_cells, dtype=jnp.int32)[:, None] == target[None, :]
    ).astype(jnp.bfloat16)
    obs_sum = lax.psum_scatter(
        jnp.dot(picks, flattened, preferred_element_type=jnp.float32),
        "lon",
        scatter_dimension=0,
        tiled=True,
    )
    obs_gradient = obs_sum.reshape(lat_cells, num_fields, lev_cells, lon_cells).transpose(
        1, 2, 0, 3
    )
    wind_pair = jnp.stack([courant_lon, courant_lat])
    joined = jnp.concatenate([adjoint_in, wind_pair], axis=0)
    widened = widen(joined, STEPS)
    adjoint = widened[:num_fields]
    for sub_step in range(STEPS):
        rim_width = STEPS - sub_step
        wind_wide = widened[
            num_fields:,
            sub_step : sub_step + lev_cells + 2 * rim_width,
            sub_step : sub_step + lat_cells + 2 * rim_width,
            sub_step : sub_step + lon_cells + 2 * rim_width,
        ]
        adjoint = sweep(
            adjoint,
            wind_wide,
            horiz_diff,
            vert_diff,
            rim_width,
            lev_first,
            lat_first,
            level_total,
            lat_total,
        )
    return adjoint + obs_gradient


def solution(mesh):
    in_specs = (
        P(None, "lev", "lat", "lon"),
        P("lev", "lat", "lon"),
        P("lev", "lat", "lon"),
        P(),
        P(),
        P(("lon", "lat"), None, "lev", None),
        P(("lon", "lat"), None, None),
        P(("lon", "lat"), None),
        P(("lon", "lat")),
        P(("lon", "lat")),
    )
    out_specs = P(None, "lev", "lat", "lon")
    return jax.shard_map(
        on_device, mesh=mesh, in_specs=in_specs, out_specs=out_specs, check_vma=False
    )
```

profile of v0, /device:TPU:1, one launch (start us, length us, event | category | flops | bytes accessed | tf_op | source)
XLA Modules:
  0.0 62.6 jit_solution(10001466940435316341)
XLA Ops:
  6.5 1.0 %pad_maximum_fusion.3 = f32[10,4,4,256]{3,2,1,0:T(4,128)S(1)} fusion(f32[1,4,4,256]{3,2,1,0:T(4,128)} %bitcast.30, f32[1,4,4,256]{3,2,1,0:T(4,128)} %bitcast.34, f32[8,4,4,256]{3,2,1,0:T(4,128)} %param.10), kind=kLoop, calls=%fused_computation.47 | loop fusion | flops 81920 | bytes 327680 | tf_op jit(solution)/shard_map/concatenate | solution.py:121
  7.6 2.1 %collective-permute-start = (f32[10,4,4,3]{3,2,1,0:T(4,128)S(1)}, f32[10,4,4,3]{3,2,1,0:T(4,128)S(1)}, u32[]{:S(2)}, u32[]{:S(2)}) collective-permute-start(f32[10,4,4,3]{3,2,1,0:T(4,128)S(1)} %get-tuple-element.27), channel_id=1, source_target_pairs={{0,16},{16,0},{1,17},{17,1},{2,18},{18,2},{3,19},{19,3},{4,20},{20... | collective-permute-start | bytes 5768 | tf_op jit(solution)/shard_map/ppermute | solution.py:16
  9.8 0.7 %iota_compare_fusion = pred[64,128]{1,0:T(8,128)(4,1)S(1)} fusion(s32[64]{0:T(128)} %param.19), kind=kLoop, calls=%fused_computation.70 | loop fusion | flops 8192 | bytes 8448 | tf_op jit(solution)/shard_map/lt | solution.py:99
  10.5 1.3 %broadcast_select_fusion = bf16[64,8,4,128]{3,2,1,0:T(4,128)(2,1)S(1)} fusion(bf16[64,8,4,128]{3,2,1,0:T(4,128)(2,1)} %param.15, pred[64,128]{1,0:T(8,128)(4,1)S(1)} %iota_compare_fusion), kind=kLoop, calls=%fused_computation.39 | loop fusion | flops 262144 | bytes 1056768 | tf_op jit(solution)/shard_map/jit(_where)/select_n | solution.py:100
  11.9 2.9 %convolution_convert_fusion = bf16[64,32,256]{2,1,0:T(8,128)(2,1)S(1)} fusion(bf16[64,32,128]{2,1,0:T(8,128)(2,1)S(1)} %bitcast.28, bf16[64,128,256]{2,1,0:T(8,128)(2,1)} %param.16), kind=kOutput, calls=%fused_computation.3 | convolution fusion | flops 134742016 | bytes 5767168 | tf_op jit(solution)/shard_map/bvo,boc->bvc/dot_general | solution.py:102
  14.8 0.6 %copy.14 = bf16[8,8,32,256]{3,1,2,0:T(8,128)(2,1)S(1)} copy(bf16[8,8,32,256]{3,2,1,0:T(8,128)(2,1)S(1)} %bitcast.27) | data formatting | bytes 2097152
  15.5 1.0 %fusion.27 = f32[8,8192]{1,0:T(8,128)} fusion(bf16[64,8192]{1,0:T(8,128)(2,1)S(1)} %bitcast.26, s32[64]{0:T(128)S(1)} %bitcast_add_fusion), kind=kOutput, calls=%fused_computation.82 | convolution fusion | flops 8389120 | bytes 1310976 | tf_op jit(solution)/shard_map/dot_general | solution.py:112
  17.6 3.4 %collective-permute-start.2 = (f32[10,4,3,262]{3,2,1,0:T(4,128)S(1)}, f32[10,4,3,262]{3,2,1,0:T(4,128)S(1)}, u32[]{:S(2)}, u32[]{:S(2)}) collective-permute-start(f32[10,4,3,262]{3,2,1,0:T(4,128)S(1)} %get-tuple-element.25), channel_id=1, source_target_pairs={{0,4},{4,8},{8,12},{1,5},{5,9},{9,13},{2,6},{6,10},{10,14},{3,7},{... | collective-permute-start | bytes 377288 | tf_op jit(solution)/shard_map/ppermute | solution.py:16
  21.0 1.3 %collective-permute-start.3 = (f32[10,4,3,262]{3,2,1,0:T(4,128)S(1)}, f32[10,4,3,262]{3,2,1,0:T(4,128)S(1)}, u32[]{:S(2)}, u32[]{:S(2)}) collective-permute-start(f32[10,4,3,262]{3,2,1,0:T(4,128)S(1)} %get-tuple-element.26), channel_id=1, source_target_pairs={{4,0},{8,4},{12,8},{5,1},{9,5},{13,9},{6,2},{10,6},{14,10},{7,3},{... | collective-permute-start | bytes 377288 | tf_op jit(solution)/shard_map/ppermute | solution.py:19
  22.4 0.6 dynamic-slice
  23.8 1.3 %collective-permute-done.2 = f32[10,4,3,262]{3,2,1,0:T(4,128)S(1)} collective-permute-done((f32[10,4,3,262]{3,2,1,0:T(4,128)S(1)}, f32[10,4,3,262]{3,2,1,0:T(4,128)S(1)}, u32[]{:S(2)}, u32[]{:S(2)}) %collective-permute-start.2) | collective-permute-done | bytes 125792 | tf_op jit(solution)/shard_map/ppermute | solution.py:16
  25.1 4.0 %collective-permute-done.3 = f32[10,4,3,262]{3,2,1,0:T(4,128)S(1)} collective-permute-done((f32[10,4,3,262]{3,2,1,0:T(4,128)S(1)}, f32[10,4,3,262]{3,2,1,0:T(4,128)S(1)}, u32[]{:S(2)}, u32[]{:S(2)}) %collective-permute-start.3) | collective-permute-done | bytes 125792 | tf_op jit(solution)/shard_map/ppermute | solution.py:19
  29.0 0.5 pad_maximum_fusion.1
  29.5 1.0 %fusion.32 = (f32[10,3,10,262]{3,2,1,0:T(8,128)}, f32[10,3,10,262]{3,2,1,0:T(8,128)S(1)}) fusion(f32[10,4,10,262]{3,2,1,0:T(8,128)S(1)} %pad_maximum_fusion.1), kind=kLoop, calls=%fused_computation.107 | loop fusion | bytes 1257600 | tf_op jit(solution)/shard_map/slice | solution.py:17
  30.5 5.3 %collective-permute-start.4 = (f32[10,3,10,262]{3,2,1,0:T(8,128)}, f32[10,3,10,262]{3,2,1,0:T(8,128)S(1)}, u32[]{:S(2)}, u32[]{:S(2)}) collective-permute-start(f32[10,3,10,262]{3,2,1,0:T(8,128)} %get-tuple-element.23), channel_id=1, source_target_pairs={{0,1},{1,2},{2,3},{4,5},{5,6},{6,7},{8,9},{9,10},{10,11},{12,13},{... | collective-permute-start | bytes 943208 | tf_op jit(solution)/shard_map/ppermute | solution.py:16
  35.8 1.9 %collective-permute-start.5 = (f32[10,3,10,262]{3,2,1,0:T(8,128)S(1)}, f32[10,3,10,262]{3,2,1,0:T(8,128)S(1)}, u32[]{:S(2)}, u32[]{:S(2)}) collective-permute-start(f32[10,3,10,262]{3,2,1,0:T(8,128)S(1)} %get-tuple-element.24), channel_id=1, source_target_pairs={{1,0},{2,1},{3,2},{5,4},{6,5},{7,6},{9,8},{10,9},{11,10},{13,12},{... | collective-permute-start | bytes 943208 | tf_op jit(solution)/shard_map/ppermute | solution.py:19
  37.8 3.7 %all-reduce.3.cloned.1.call-done = f32[8,8192]{1,0:T(8,128)} async-done(((f32[8,8192]{1,0:T(8,128)}), f32[8,8192]{1,0:T(8,128)}) %all-reduce.3.cloned.1.call-update) | async-done | bytes 262160
  41.5 1.0 %constant_dynamic-slice_fusion = f32[4,8192]{1,0:T(4,128)S(1)} fusion(f32[8,8192]{1,0:T(8,128)} %all-reduce.3.cloned.1.call-done, u32[]{:T(128)S(6)} %multiply.1), kind=kLoop, calls=%fused_computation.98 | loop fusion | bytes 262148
  42.4 2.1 %collective-permute-done.4 = f32[10,3,10,262]{3,2,1,0:T(8,128)S(1)} collective-permute-done((f32[10,3,10,262]{3,2,1,0:T(8,128)}, f32[10,3,10,262]{3,2,1,0:T(8,128)S(1)}, u32[]{:S(2)}, u32[]{:S(2)}) %collective-permute-start.4) | collective-permute-done | bytes 314432 | tf_op jit(solution)/shard_map/ppermute | solution.py:16
  44.5 4.1 %collective-permute-done.5 = f32[10,3,10,262]{3,2,1,0:T(8,128)S(1)} collective-permute-done((f32[10,3,10,262]{3,2,1,0:T(8,128)S(1)}, f32[10,3,10,262]{3,2,1,0:T(8,128)S(1)}, u32[]{:S(2)}, u32[]{:S(2)}) %collective-permute-start.5) | collective-permute-done | bytes 314432 | tf_op jit(solution)/shard_map/ppermute | solution.py:19
  48.6 0.6 pad_maximum_fusion
  50.1 2.3 %broadcast_multiply_fusion.1 = (f32[8,8,8,260]{3,2,1,0:T(8,128)S(1)}, f32[8,8,8,260]{3,2,1,0:T(8,128)S(1)}) fusion(f32[8,8,260]{2,1,0:T(8,128)S(1)} %get-tuple-element.18, f32[8,8]{1,0:T(8,128)S(1)} %and_convert_fusion.1, f32[10,10,10,262]{3,2,1,0:T(8,128)S(1)} %pad_maximum_fusion, f32[8]{0:T(128)S(1)} %get-tuple-element.10, f32[8]{0:T(128)S(1)} %get-tuple-element.9, ...), kind=kLoop, calls=%fused_computation.41 | loop fusion | flops 2529280 | bytes 6989152 | tf_op jit(solution)/shard_map/mul | solution.py:59
  52.5 1.7 %broadcast_multiply_fusion.3 = (f32[8,6,6,258]{3,2,1,0:T(8,128)S(1)}, f32[8,6,6,258]{3,2,1,0:T(8,128)S(1)}) fusion(f32[6,6,258]{2,1,0:T(8,128)S(1)} %get-tuple-element.16, f32[6,6]{1,0:T(8,128)S(1)} %and_convert_fusion, f32[8,8,8,260]{3,2,1,0:T(8,128)S(1)} %get-tuple-element.14, f32[6]{0:T(128)S(1)} %get-tuple-element.8, f32[6]{0:T(128)S(1)} %get-tuple-element.7, ...), kind=kLoop, calls=%fused_computation.43 | loop fusion | flops 1411776 | bytes 3901184 | tf_op jit(solution)/shard_map/mul | solution.py:59
  54.3 1.4 %fusion.19 = f32[8,4,4,256]{3,2,1,0:T(4,128)} fusion(f32[8,4,4,256]{3,2,1,0:T(4,128)S(1)} %bitcast.29, f32[8,6,6,258]{3,2,1,0:T(8,128)S(1)} %get-tuple-element.12, f32[8,6,6,258]{3,2,1,0:T(8,128)S(1)} %broadcast_multiply_fusion.2, f32[8,6,6,258]{3,2,1,0:T(8,128)S(1)} %get-tuple-element.11, f32[4,4]{1,0:T(4,128)S(1)} %and_convert_fusion.2, ...), kind=kLoop, calls=%fused_computation.52 | loop fusion | flops 622592 | bytes 1704064 | tf_op jit(solution)/shard_map/add | solution.py:143
  (44 shorter events, 2.5 us)
Async XLA Ops:
  6.5 34.9 %all-reduce.3.cloned.1.call-start = ((), (), s32[]{:S(2)}) async-start(), calls=%async_computation | async-start | bytes 524288
  7.6 9.6 %collective-permute-start = (f32[10,4,4,3]{3,2,1,0:T(4,128)S(1)}, f32[10,4,4,3]{3,2,1,0:T(4,128)S(1)}, u32[]{:S(2)}, u32[]{:S(2)}) collective-permute-start(f32[10,4,4,3]{3,2,1,0:T(4,128)S(1)} %get-tuple-element.27), channel_id=1, source_target_pairs={{0,16},{16,0},{1,17},{17,1},{2,18},{18,2},{3,19},{19,3},{4,20},{20... | collective-permute-start | bytes 5768 | tf_op jit(solution)/shard_map/ppermute | solution.py:16
  9.7 7.5 %collective-permute-start.1 = (f32[10,4,4,3]{3,2,1,0:T(4,128)S(1)}, f32[10,4,4,3]{3,2,1,0:T(4,128)S(1)}, u32[]{:S(2)}, u32[]{:S(2)}) collective-permute-start(f32[10,4,4,3]{3,2,1,0:T(4,128)S(1)} %get-tuple-element.28), channel_id=1, source_target_pairs={{16,0},{0,16},{17,1},{1,17},{18,2},{2,18},{19,3},{3,19},{20,4},{4,... | collective-permute-start | bytes 5768 | tf_op jit(solution)/shard_map/ppermute | solution.py:19
  11.8 3.6 %copy-start.5 = (s32[64]{0:T(128)S(1)}, s32[64]{0:T(128)}, u32[]{:S(2)}) copy-start(s32[64]{0:T(128)} %param.18) | copy-start | bytes 772
  11.8 3.6 %copy-start.6 = (s32[64,1]{0,1:T(1,128)S(1)}, s32[64,1]{0,1:T(1,128)}, u32[]{:S(2)}) copy-start(s32[64,1]{0,1:T(1,128)} %param.17) | copy-start | bytes 772
  14.8 2.0 %copy-start.4 = (f32[16]{0:T(128)S(1)}, f32[16]{0:T(128)}, u32[]{:S(2)}) copy-start(f32[16]{0:T(128)} %param.14) | copy-start | bytes 196
  14.8 2.5 %copy-start = (f32[8,4,4,256]{3,2,1,0:T(4,128)S(1)}, f32[8,4,4,256]{3,2,1,0:T(4,128)}, u32[]{:S(2)}) copy-start(f32[8,4,4,256]{3,2,1,0:T(4,128)} %param.10) | copy-start | bytes 393220
  14.8 2.5 %copy-start.1 = (f32[4,4,256]{2,1,0:T(4,128)S(1)}, f32[4,4,256]{2,1,0:T(4,128)}, u32[]{:S(2)}) copy-start(f32[4,4,256]{2,1,0:T(4,128)} %param.12) | copy-start | bytes 49156
  14.8 2.5 %copy-start.2 = (f32[4,4,256]{2,1,0:T(4,128)S(1)}, f32[4,4,256]{2,1,0:T(4,128)}, u32[]{:S(2)}) copy-start(f32[4,4,256]{2,1,0:T(4,128)} %param.11) | copy-start | bytes 49156
  14.8 7.5 %copy-start.7 = (u32[32]{0:T(128)S(1)}, u32[32]{0:T(128)}, u32[]{:S(2)}) copy-start(u32[32]{0:T(128)} %constant.44) | copy-start | bytes 388
  17.6 7.4 %collective-permute-start.2 = (f32[10,4,3,262]{3,2,1,0:T(4,128)S(1)}, f32[10,4,3,262]{3,2,1,0:T(4,128)S(1)}, u32[]{:S(2)}, u32[]{:S(2)}) collective-permute-start(f32[10,4,3,262]{3,2,1,0:T(4,128)S(1)} %get-tuple-element.25), channel_id=1, source_target_pairs={{0,4},{4,8},{8,12},{1,5},{5,9},{9,13},{2,6},{6,10},{10,14},{3,7},{... | collective-permute-start | bytes 377288 | tf_op jit(solution)/shard_map/ppermute | solution.py:16
  21.0 8.0 %collective-permute-start.3 = (f32[10,4,3,262]{3,2,1,0:T(4,128)S(1)}, f32[10,4,3,262]{3,2,1,0:T(4,128)S(1)}, u32[]{:S(2)}, u32[]{:S(2)}) collective-permute-start(f32[10,4,3,262]{3,2,1,0:T(4,128)S(1)} %get-tuple-element.26), channel_id=1, source_target_pairs={{4,0},{8,4},{12,8},{5,1},{9,5},{13,9},{6,2},{10,6},{14,10},{7,3},{... | collective-permute-start | bytes 377288 | tf_op jit(solution)/shard_map/ppermute | solution.py:19
  30.5 14.0 %collective-permute-start.4 = (f32[10,3,10,262]{3,2,1,0:T(8,128)}, f32[10,3,10,262]{3,2,1,0:T(8,128)S(1)}, u32[]{:S(2)}, u32[]{:S(2)}) collective-permute-start(f32[10,3,10,262]{3,2,1,0:T(8,128)} %get-tuple-element.23), channel_id=1, source_target_pairs={{0,1},{1,2},{2,3},{4,5},{5,6},{6,7},{8,9},{9,10},{10,11},{12,13},{... | collective-permute-start | bytes 943208 | tf_op jit(solution)/shard_map/ppermute | solution.py:16
  35.8 12.8 %collective-permute-start.5 = (f32[10,3,10,262]{3,2,1,0:T(8,128)S(1)}, f32[10,3,10,262]{3,2,1,0:T(8,128)S(1)}, u32[]{:S(2)}, u32[]{:S(2)}) collective-permute-start(f32[10,3,10,262]{3,2,1,0:T(8,128)S(1)} %get-tuple-element.24), channel_id=1, source_target_pairs={{1,0},{2,1},{3,2},{5,4},{6,5},{7,6},{9,8},{10,9},{11,10},{13,12},{... | collective-permute-start | bytes 943208 | tf_op jit(solution)/shard_map/ppermute | solution.py:19
  49.5 0.7 %copy-start.3 = (f32[8]{0:T(128)S(1)}, f32[8]{0:T(128)}, u32[]{:S(2)}) copy-start(f32[8]{0:T(128)} %param.13) | copy-start | bytes 100
Sparse Core Ops, SparseCore 0:
  16.6 24.8 all-reduce.2
where the time goes:
time: 62.9 us; the launch traced here: 62.6 us
  waiting for transfers between devices  15.1 us (24%)
  between operations  14.4 us (23%)
  starting transfers between devices  14.1 us (22%)
  other arithmetic  11.2 us (18%)
  local copies, waits for them, and re-layouts  3.92 us (6%)
  matrix products  3.87 us (6%)
    ppermute x3, starting transfers between devices, extended_2(): lax.ppermute(lax.slice_in_dim(block, block.shape[dim] - width, None, axis...  10.8 us
    ppermute x3, waiting for transfers between devices, extended_2(): lax.ppermute(lax.slice_in_dim(block, 0, width, axis=dim), axis, backward)  8.03 us
    mul x3, other arithmetic, sweep(): east_flux = wind_pair[0][None] * extended  4.4 us
    unnamed x2, waiting for transfers between devices  3.73 us
    ppermute x3, waiting for transfers between devices, extended_2(): lax.ppermute(lax.slice_in_dim(block, block.shape[dim] - width, None, axis...  3.36 us
    ppermute x3, starting transfers between devices, extended_2(): lax.ppermute(lax.slice_in_dim(block, 0, width, axis=dim), axis, backward)  3.29 us
    dot_general x1, matrix products, on_device(): jnp.einsum('bvo,boc->bvc', masked, obs_operator, preferred_element_type=j...  2.91 us
    unnamed x19, local copies, waits for them, and re-layouts  2.48 us
  transfers between devices with their start and end apart: 7, of which 5 were waited for; matrix products, arithmetic and copies ran while one was open for 17% of the time, Pallas kernels for 0%

commit v1 on v0

--- a/solution.py
+++ b/solution.py
@@ -108,12 +108,14 @@
     picks = (
         jnp.arange(lax.axis_size("lon") * lat_cells, dtype=jnp.int32)[:, None] == target[None, :]
     ).astype(jnp.bfloat16)
-    obs_sum = lax.psum_scatter(
-        jnp.dot(picks, flattened, preferred_element_type=jnp.float32),
-        "lon",
-        scatter_dimension=0,
-        tiled=True,
-    )
+    partial_sums = jnp.dot(picks, flattened, preferred_element_type=jnp.float32)
+    if lax.axis_size("lon") == 2:
+        my_lon = lax.axis_index("lon")
+        mine = lax.dynamic_slice_in_dim(partial_sums, my_lon * lat_cells, lat_cells, 0)
+        other = lax.dynamic_slice_in_dim(partial_sums, (1 - my_lon) * lat_cells, lat_cells, 0)
+        obs_sum = mine + lax.ppermute(other, "lon", [(0, 1), (1, 0)])
+    else:
+        obs_sum = lax.psum_scatter(partial_sums, "lon", scatter_dimension=0, tiled=True)
     obs_gradient = obs_sum.reshape(lat_cells, num_fields, lev_cells, lon_cells).transpose(
         1, 2, 0, 3
     )

time: 62.9 us -> 49.1 us (0.78)
  between operations: 14.4 us -> 0.34 us
  local copies, waits for them, and re-layouts: 3.92 us -> 1.5 us
  waiting for transfers between devices: 15.1 us -> 16.9 us
  starting transfers between devices: 14.1 us -> 15.7 us
  matrix products: 3.87 us -> 3.16 us
    ppermute x3, waiting for transfers between devices: 3.36 us -> 8.64 us  [extended_2(): lax.ppermute(lax.slice_in_dim(block, block.shape[dim] - width, None, axis...]
    unnamed x2 -> x0, waiting for transfers between devices: 3.73 us -> none
    unnamed x19 -> x15, local copies, waits for them, and re-layouts: 2.48 us -> 0.91 us
    ppermute x0 -> x1, starting transfers between devices: none -> 1.45 us  [on_device(): obs_sum = mine + lax.ppermute(other, 'lon', [(0, 1), (1, 0)])]
    slice x3, local copies, waits for them, and re-layouts: 1.19 us -> 0.31 us  [extended_2(): lax.slice_in_dim(block, block.shape[dim] - width, None, axis=dim)]
    dot_general x1, matrix products: 0.96 us -> 0.25 us  [on_device(): partial_sums = jnp.dot(picks, flattened, preferred_element_type=jnp.float32)]
  transfers between devices with their start and end apart: 7 -> 7, of which waited for: 5 -> 4; matrix products, arithmetic and copies ran while one was open for 17% -> 16% of each run, Pallas kernels for 0% -> 0%
where the time goes in v1:
time: 49.1 us; the launch traced here: 48.9 us
  waiting for transfers between devices  16.9 us (34%)
  starting transfers between devices  15.7 us (32%)
  other arithmetic  11.2 us (23%)
  matrix products  3.16 us (6%)
  local copies, waits for them, and re-layouts  1.5 us (3%)
    ppermute x3, starting transfers between devices, extended_2(): lax.ppermute(lax.slice_in_dim(block, block.shape[dim] - width, None, axis...  11 us
    ppermute x3, waiting for transfers between devices, extended_2(): lax.ppermute(lax.slice_in_dim(block, block.shape[dim] - width, None, axis...  8.64 us
    ppermute x3, waiting for transfers between devices, extended_2(): lax.ppermute(lax.slice_in_dim(block, 0, width, axis=dim), axis, backward)  8.24 us
    mul x3, other arithmetic, sweep(): east_flux = wind_pair[0][None] * extended  4.4 us
    ppermute x3, starting transfers between devices, extended_2(): lax.ppermute(lax.slice_in_dim(block, 0, width, axis=dim), axis, backward)  3.29 us
    dot_general x1, matrix products, on_device(): jnp.einsum('bvo,boc->bvc', masked, obs_operator, preferred_element_type=j...  2.91 us
    ppermute x1, starting transfers between devices, on_device(): obs_sum = mine + lax.ppermute(other, 'lon', [(0, 1), (1, 0)])  1.45 us
    add x1, other arithmetic, on_device(): return adjoint + obs_gradient  1.45 us
  transfers between devices with their start and end apart: 7, of which 4 were waited for; matrix products, arithmetic and copies ran while one was open for 16% of the time, Pallas kernels for 0%

profile of v1, /device:TPU:1, one launch (start us, length us, event | category | flops | bytes accessed | tf_op | source)
XLA Modules:
  0.0 48.9 jit_solution(14239155979865314943)
XLA Ops:
  0.0 1.0 %pad_maximum_fusion.3 = f32[10,4,4,256]{3,2,1,0:T(4,128)S(1)} fusion(f32[1,4,4,256]{3,2,1,0:T(4,128)} %bitcast.29, f32[1,4,4,256]{3,2,1,0:T(4,128)} %bitcast.33, f32[8,4,4,256]{3,2,1,0:T(4,128)} %param.10), kind=kLoop, calls=%fused_computation.47 | loop fusion | flops 81920 | bytes 327680 | tf_op jit(solution)/shard_map/concatenate | solution.py:123
  1.1 2.1 %collective-permute-start = (f32[10,4,4,3]{3,2,1,0:T(4,128)S(1)}, f32[10,4,4,3]{3,2,1,0:T(4,128)S(1)}, u32[]{:S(2)}, u32[]{:S(2)}) collective-permute-start(f32[10,4,4,3]{3,2,1,0:T(4,128)S(1)} %get-tuple-element.27), channel_id=1, source_target_pairs={{0,16},{16,0},{1,17},{17,1},{2,18},{18,2},{3,19},{19,3},{4,20},{20... | collective-permute-start | bytes 5768 | tf_op jit(solution)/shard_map/ppermute | solution.py:16
  3.3 0.7 %iota_compare_fusion = pred[64,128]{1,0:T(8,128)(4,1)S(1)} fusion(s32[64]{0:T(128)} %param.19), kind=kLoop, calls=%fused_computation.71 | loop fusion | flops 8192 | bytes 8448 | tf_op jit(solution)/shard_map/lt | solution.py:99
  4.0 1.3 %broadcast_select_fusion = bf16[64,8,4,128]{3,2,1,0:T(4,128)(2,1)S(1)} fusion(bf16[64,8,4,128]{3,2,1,0:T(4,128)(2,1)} %param.15, pred[64,128]{1,0:T(8,128)(4,1)S(1)} %iota_compare_fusion), kind=kLoop, calls=%fused_computation.39 | loop fusion | flops 262144 | bytes 1056768 | tf_op jit(solution)/shard_map/jit(_where)/select_n | solution.py:100
  5.3 2.9 %convolution_convert_fusion = bf16[64,32,256]{2,1,0:T(8,128)(2,1)S(1)} fusion(bf16[64,32,128]{2,1,0:T(8,128)(2,1)S(1)} %bitcast.27, bf16[64,128,256]{2,1,0:T(8,128)(2,1)} %param.16), kind=kOutput, calls=%fused_computation.3 | convolution fusion | flops 134742016 | bytes 5767168 | tf_op jit(solution)/shard_map/bvo,boc->bvc/dot_general | solution.py:102
  8.3 0.6 %copy.13 = bf16[8,8,32,256]{3,1,2,0:T(8,128)(2,1)S(1)} copy(bf16[8,8,32,256]{3,2,1,0:T(8,128)(2,1)S(1)} %bitcast.26) | data formatting | bytes 2097152
  8.9 0.2 fusion.27
  9.2 1.5 %collective-permute-start.6 = (f32[4,8192]{1,0:T(4,128)S(1)}, f32[4,8192]{1,0:T(4,128)S(1)}, u32[]{:S(2)}, u32[]{:S(2)}) collective-permute-start(f32[4,8192]{1,0:T(4,128)S(1)} %constant_dynamic-slice_fusion), channel_id=1, source_target_pairs={{0,16},{16,0},{1,17},{17,1},{2,18},{18,2},{3,19},{19,3},{4,20},{20... | collective-permute-start | bytes 393224 | tf_op jit(solution)/shard_map/ppermute | solution.py:116
  11.5 0.2 pad_maximum_fusion.2
  11.8 3.2 %collective-permute-start.2 = (f32[10,4,3,262]{3,2,1,0:T(4,128)S(1)}, f32[10,4,3,262]{3,2,1,0:T(4,128)S(1)}, u32[]{:S(2)}, u32[]{:S(2)}) collective-permute-start(f32[10,4,3,262]{3,2,1,0:T(4,128)S(1)} %get-tuple-element.25), channel_id=1, source_target_pairs={{0,4},{4,8},{8,12},{1,5},{5,9},{9,13},{2,6},{6,10},{10,14},{3,7},{... | collective-permute-start | bytes 377288 | tf_op jit(solution)/shard_map/ppermute | solution.py:16
  15.0 1.3 %collective-permute-start.3 = (f32[10,4,3,262]{3,2,1,0:T(4,128)S(1)}, f32[10,4,3,262]{3,2,1,0:T(4,128)S(1)}, u32[]{:S(2)}, u32[]{:S(2)}) collective-permute-start(f32[10,4,3,262]{3,2,1,0:T(4,128)S(1)} %get-tuple-element.26), channel_id=1, source_target_pairs={{4,0},{8,4},{12,8},{5,1},{9,5},{13,9},{6,2},{10,6},{14,10},{7,3},{... | collective-permute-start | bytes 377288 | tf_op jit(solution)/shard_map/ppermute | solution.py:19
  16.6 2.2 %collective-permute-done.2 = f32[10,4,3,262]{3,2,1,0:T(4,128)S(1)} collective-permute-done((f32[10,4,3,262]{3,2,1,0:T(4,128)S(1)}, f32[10,4,3,262]{3,2,1,0:T(4,128)S(1)}, u32[]{:S(2)}, u32[]{:S(2)}) %collective-permute-start.2) | collective-permute-done | bytes 125792 | tf_op jit(solution)/shard_map/ppermute | solution.py:16
  18.8 3.8 %collective-permute-done.3 = f32[10,4,3,262]{3,2,1,0:T(4,128)S(1)} collective-permute-done((f32[10,4,3,262]{3,2,1,0:T(4,128)S(1)}, f32[10,4,3,262]{3,2,1,0:T(4,128)S(1)}, u32[]{:S(2)}, u32[]{:S(2)}) %collective-permute-start.3) | collective-permute-done | bytes 125792 | tf_op jit(solution)/shard_map/ppermute | solution.py:19
  22.7 0.5 %pad_maximum_fusion.1 = f32[10,4,10,262]{3,2,1,0:T(8,128)S(1)} fusion(f32[10,4,3,262]{3,2,1,0:T(4,128)S(1)} %collective-permute-done.3, f32[10,4,4,3]{3,2,1,0:T(4,128)S(1)} %collective-permute-done.1, f32[1,4,4,256]{3,2,1,0:T(4,128)S(1)} %bitcast.31, f32[1,4,4,256]{3,2,1,0:T(4,128)S(1)} %bitcast.35, f32[8,4,4,256]{3,2,1,0:T(4,128)S(1)} %copy-done, ...), kind=kLoop, calls=%fused_computation.4 | loop fusion | flops 628800 | bytes 838400 | tf_op jit(solution)/shard_map/concatenate | solution.py:20
  23.3 5.7 %collective-permute-start.4 = (f32[10,3,10,262]{3,2,1,0:T(8,128)S(1)}, f32[10,3,10,262]{3,2,1,0:T(8,128)S(1)}, u32[]{:S(2)}, u32[]{:S(2)}) collective-permute-start(f32[10,3,10,262]{3,2,1,0:T(8,128)S(1)} %get-tuple-element.23), channel_id=1, source_target_pairs={{0,1},{1,2},{2,3},{4,5},{5,6},{6,7},{8,9},{9,10},{10,11},{12,13},{... | collective-permute-start | bytes 943208 | tf_op jit(solution)/shard_map/ppermute | solution.py:16
  29.0 1.9 %collective-permute-start.5 = (f32[10,3,10,262]{3,2,1,0:T(8,128)S(1)}, f32[10,3,10,262]{3,2,1,0:T(8,128)S(1)}, u32[]{:S(2)}, u32[]{:S(2)}) collective-permute-start(f32[10,3,10,262]{3,2,1,0:T(8,128)S(1)} %get-tuple-element.24), channel_id=1, source_target_pairs={{1,0},{2,1},{3,2},{5,4},{6,5},{7,6},{9,8},{10,9},{11,10},{13,12},{... | collective-permute-start | bytes 943208 | tf_op jit(solution)/shard_map/ppermute | solution.py:19
  31.0 6.4 %collective-permute-done.4 = f32[10,3,10,262]{3,2,1,0:T(8,128)S(1)} collective-permute-done((f32[10,3,10,262]{3,2,1,0:T(8,128)S(1)}, f32[10,3,10,262]{3,2,1,0:T(8,128)S(1)}, u32[]{:S(2)}, u32[]{:S(2)}) %collective-permute-start.4) | collective-permute-done | bytes 314432 | tf_op jit(solution)/shard_map/ppermute | solution.py:16
  37.4 4.4 %collective-permute-done.5 = f32[10,3,10,262]{3,2,1,0:T(8,128)S(1)} collective-permute-done((f32[10,3,10,262]{3,2,1,0:T(8,128)S(1)}, f32[10,3,10,262]{3,2,1,0:T(8,128)S(1)}, u32[]{:S(2)}, u32[]{:S(2)}) %collective-permute-start.5) | collective-permute-done | bytes 314432 | tf_op jit(solution)/shard_map/ppermute | solution.py:19
  41.7 0.6 %pad_maximum_fusion = f32[10,10,10,262]{3,2,1,0:T(8,128)S(1)} fusion(f32[10,3,10,262]{3,2,1,0:T(8,128)S(1)} %collective-permute-done.5, f32[10,4,3,262]{3,2,1,0:T(4,128)S(1)} %collective-permute-done.3, f32[10,4,4,3]{3,2,1,0:T(4,128)S(1)} %collective-permute-done.1, f32[1,4,4,256]{3,2,1,0:T(4,128)S(1)} %bitcast.32, f32[1,4,4,256]{3,2,1,0:T(4,128)S(1)} %bitcast.36, ...), kind=kLoop, calls=%fused_computation | loop fusion | flops 2096000 | bytes 2096000 | tf_op jit(solution)/shard_map/concatenate | solution.py:20
  42.6 0.4 slice_multiply_fusion.1
  43.0 0.2 copy-done.3
  43.3 2.3 %broadcast_multiply_fusion.1 = (f32[8,8,8,260]{3,2,1,0:T(8,128)S(1)}, f32[8,8,8,260]{3,2,1,0:T(8,128)S(1)}) fusion(f32[8,8,260]{2,1,0:T(8,128)S(1)} %get-tuple-element.18, f32[8,8]{1,0:T(8,128)S(1)} %and_convert_fusion.1, f32[10,10,10,262]{3,2,1,0:T(8,128)S(1)} %pad_maximum_fusion, f32[8]{0:T(128)S(1)} %get-tuple-element.10, f32[8]{0:T(128)S(1)} %get-tuple-element.9, ...), kind=kLoop, calls=%fused_computation.41 | loop fusion | flops 2529280 | bytes 6989152 | tf_op jit(solution)/shard_map/mul | solution.py:59
  45.6 1.7 %broadcast_multiply_fusion.3 = (f32[8,6,6,258]{3,2,1,0:T(8,128)S(1)}, f32[8,6,6,258]{3,2,1,0:T(8,128)S(1)}) fusion(f32[6,6,258]{2,1,0:T(8,128)S(1)} %get-tuple-element.16, f32[6,6]{1,0:T(8,128)S(1)} %and_convert_fusion, f32[8,8,8,260]{3,2,1,0:T(8,128)S(1)} %get-tuple-element.14, f32[6]{0:T(128)S(1)} %get-tuple-element.8, f32[6]{0:T(128)S(1)} %get-tuple-element.7, ...), kind=kLoop, calls=%fused_computation.43 | loop fusion | flops 1411776 | bytes 3901184 | tf_op jit(solution)/shard_map/mul | solution.py:59
  47.4 1.4 %fusion.19 = f32[8,4,4,256]{3,2,1,0:T(4,128)} fusion(f32[8,4,4,256]{3,2,1,0:T(4,128)S(1)} %bitcast.28, f32[8,6,6,258]{3,2,1,0:T(8,128)S(1)} %get-tuple-element.12, f32[8,6,6,258]{3,2,1,0:T(8,128)S(1)} %broadcast_multiply_fusion.2, f32[8,6,6,258]{3,2,1,0:T(8,128)S(1)} %get-tuple-element.11, f32[4,4]{1,0:T(4,128)S(1)} %and_convert_fusion.2, ...), kind=kLoop, calls=%fused_computation.52 | loop fusion | flops 622592 | bytes 1704064 | tf_op jit(solution)/shard_map/add | solution.py:145
  (41 shorter events, 1.8 us)
Async XLA Ops:
  1.1 10.3 %collective-permute-start = (f32[10,4,4,3]{3,2,1,0:T(4,128)S(1)}, f32[10,4,4,3]{3,2,1,0:T(4,128)S(1)}, u32[]{:S(2)}, u32[]{:S(2)}) collective-permute-start(f32[10,4,4,3]{3,2,1,0:T(4,128)S(1)} %get-tuple-element.27), channel_id=1, source_target_pairs={{0,16},{16,0},{1,17},{17,1},{2,18},{18,2},{3,19},{19,3},{4,20},{20... | collective-permute-start | bytes 5768 | tf_op jit(solution)/shard_map/ppermute | solution.py:16
  3.2 8.2 %collective-permute-start.1 = (f32[10,4,4,3]{3,2,1,0:T(4,128)S(1)}, f32[10,4,4,3]{3,2,1,0:T(4,128)S(1)}, u32[]{:S(2)}, u32[]{:S(2)}) collective-permute-start(f32[10,4,4,3]{3,2,1,0:T(4,128)S(1)} %get-tuple-element.28), channel_id=1, source_target_pairs={{16,0},{0,16},{17,1},{1,17},{18,2},{2,18},{19,3},{3,19},{20,4},{4,... | collective-permute-start | bytes 5768 | tf_op jit(solution)/shard_map/ppermute | solution.py:19
  5.3 3.6 %copy-start.5 = (s32[64]{0:T(128)S(1)}, s32[64]{0:T(128)}, u32[]{:S(2)}) copy-start(s32[64]{0:T(128)} %param.18) | copy-start | bytes 772
  5.3 3.6 %copy-start.6 = (s32[64,1]{0,1:T(1,128)S(1)}, s32[64,1]{0,1:T(1,128)}, u32[]{:S(2)}) copy-start(s32[64,1]{0,1:T(1,128)} %param.17) | copy-start | bytes 772
  8.2 2.8 %copy-start.4 = (f32[16]{0:T(128)S(1)}, f32[16]{0:T(128)}, u32[]{:S(2)}) copy-start(f32[16]{0:T(128)} %param.14) | copy-start | bytes 196
  8.2 3.2 %copy-start = (f32[8,4,4,256]{3,2,1,0:T(4,128)S(1)}, f32[8,4,4,256]{3,2,1,0:T(4,128)}, u32[]{:S(2)}) copy-start(f32[8,4,4,256]{3,2,1,0:T(4,128)} %param.10) | copy-start | bytes 393220
  8.3 3.2 %copy-start.1 = (f32[4,4,256]{2,1,0:T(4,128)S(1)}, f32[4,4,256]{2,1,0:T(4,128)}, u32[]{:S(2)}) copy-start(f32[4,4,256]{2,1,0:T(4,128)} %param.12) | copy-start | bytes 49156
  8.3 3.2 %copy-start.2 = (f32[4,4,256]{2,1,0:T(4,128)S(1)}, f32[4,4,256]{2,1,0:T(4,128)}, u32[]{:S(2)}) copy-start(f32[4,4,256]{2,1,0:T(4,128)} %param.11) | copy-start | bytes 49156
  9.2 21.7 %collective-permute-start.6 = (f32[4,8192]{1,0:T(4,128)S(1)}, f32[4,8192]{1,0:T(4,128)S(1)}, u32[]{:S(2)}, u32[]{:S(2)}) collective-permute-start(f32[4,8192]{1,0:T(4,128)S(1)} %constant_dynamic-slice_fusion), channel_id=1, source_target_pairs={{0,16},{16,0},{1,17},{17,1},{2,18},{18,2},{3,19},{19,3},{4,20},{20... | collective-permute-start | bytes 393224 | tf_op jit(solution)/shard_map/ppermute | solution.py:116
  11.8 7.0 %collective-permute-start.2 = (f32[10,4,3,262]{3,2,1,0:T(4,128)S(1)}, f32[10,4,3,262]{3,2,1,0:T(4,128)S(1)}, u32[]{:S(2)}, u32[]{:S(2)}) collective-permute-start(f32[10,4,3,262]{3,2,1,0:T(4,128)S(1)} %get-tuple-element.25), channel_id=1, source_target_pairs={{0,4},{4,8},{8,12},{1,5},{5,9},{9,13},{2,6},{6,10},{10,14},{3,7},{... | collective-permute-start | bytes 377288 | tf_op jit(solution)/shard_map/ppermute | solution.py:16
  15.0 7.6 %collective-permute-start.3 = (f32[10,4,3,262]{3,2,1,0:T(4,128)S(1)}, f32[10,4,3,262]{3,2,1,0:T(4,128)S(1)}, u32[]{:S(2)}, u32[]{:S(2)}) collective-permute-start(f32[10,4,3,262]{3,2,1,0:T(4,128)S(1)} %get-tuple-element.26), channel_id=1, source_target_pairs={{4,0},{8,4},{12,8},{5,1},{9,5},{13,9},{6,2},{10,6},{14,10},{7,3},{... | collective-permute-start | bytes 377288 | tf_op jit(solution)/shard_map/ppermute | solution.py:19
  23.3 14.1 %collective-permute-start.4 = (f32[10,3,10,262]{3,2,1,0:T(8,128)S(1)}, f32[10,3,10,262]{3,2,1,0:T(8,128)S(1)}, u32[]{:S(2)}, u32[]{:S(2)}) collective-permute-start(f32[10,3,10,262]{3,2,1,0:T(8,128)S(1)} %get-tuple-element.23), channel_id=1, source_target_pairs={{0,1},{1,2},{2,3},{4,5},{5,6},{6,7},{8,9},{9,10},{10,11},{12,13},{... | collective-permute-start | bytes 943208 | tf_op jit(solution)/shard_map/ppermute | solution.py:16
  29.0 12.8 %collective-permute-start.5 = (f32[10,3,10,262]{3,2,1,0:T(8,128)S(1)}, f32[10,3,10,262]{3,2,1,0:T(8,128)S(1)}, u32[]{:S(2)}, u32[]{:S(2)}) collective-permute-start(f32[10,3,10,262]{3,2,1,0:T(8,128)S(1)} %get-tuple-element.24), channel_id=1, source_target_pairs={{1,0},{2,1},{3,2},{5,4},{6,5},{7,6},{9,8},{10,9},{11,10},{13,12},{... | collective-permute-start | bytes 943208 | tf_op jit(solution)/shard_map/ppermute | solution.py:19
  42.6 0.7 %copy-start.3 = (f32[8]{0:T(128)S(1)}, f32[8]{0:T(128)}, u32[]{:S(2)}) copy-start(f32[8]{0:T(128)} %param.13) | copy-start | bytes 100

commit v2 on v1

v2 whole, which is shorter than its diff:
```python
import functools

import jax
import jax.numpy as jnp
from jax import lax
from jax.experimental import pallas as pl
from jax.experimental.pallas import tpu as pltpu
from jax.sharding import PartitionSpec as P

STEPS = 3
LANES = 128
GROUP = 16
PER_TILE = LANES // GROUP
VMEM = pl.BlockSpec(memory_space=pltpu.VMEM)
SMEM = pl.BlockSpec(memory_space=pltpu.SMEM)
ANY = pl.BlockSpec(memory_space=pl.ANY)
HBM = pl.BlockSpec(memory_space=pltpu.HBM)


PARAMS = pltpu.CompilerParams(vmem_limit_bytes=12 << 20)


def cost(flops, nbytes):
    return pl.CostEstimate(flops=flops, bytes_accessed=nbytes, transcendentals=0)


def pair_up(count, phase, others, major):
    pairs = []
    for i in range(count):
        mate = i + 1 if i % 2 == phase else i - 1
        for j in range(others):
            to = (mate, j) if 0 <= mate < count else (i, j ^ 1)
            if to[1] < others:
                ends = [p * others + q if major else q * count + p for p, q in ((i, j), to)]
                pairs.append(tuple(ends))
    return pairs


def lev_rows(lat_cells):
    return [(d, -(STEPS - d), lat_cells + 2 * (STEPS - d)) for d in range(1, STEPS + 1)]


def load_kernel(adj, wind_u, wind_w, *refs):
    small, (own, to_a, to_b), small_out, sem = refs[:3], refs[3:6], refs[6:9], refs[9]
    fields, levs, lats = adj.shape[:3]
    copies = [
        pltpu.make_async_copy(adj.at[f], own.at[:, 0:lats, f, :], sem.at[f]) for f in range(fields)
    ]
    copies.append(pltpu.make_async_copy(wind_u, own.at[:, lats, 0:lats, :], sem.at[fields]))
    copies.append(
        pltpu.make_async_copy(wind_w, own.at[:, lats, lats : 2 * lats, :], sem.at[fields + 1])
    )
    for n, (source, target) in enumerate(zip(small, small_out)):
        copies.append(pltpu.make_async_copy(source, target, sem.at[fields + 2 + n]))
    for copy in copies:
        copy.start()
    for copy in copies:
        copy.wait()
    odd = lax.rem(lax.axis_index("lat"), 2)
    for out, start in ((to_a, (1 - odd) * (lats - STEPS)), (to_b, odd * (lats - STEPS))):
        for lev in range(levs):
            for row in range(STEPS):
                out[lev, row] = own[lev, start + row].astype(jnp.bfloat16)
            out[lev, STEPS] = own[lev, lats].astype(jnp.bfloat16)


def obs_kernel(lats, owner, block_row, count, innov, oper, *refs):
    outs, acc = refs[:-1], refs[-1]
    step = pl.program_id(0)
    blocks = oper.shape[0]
    rows = innov.shape[0] // blocks
    fields = 8
    levs = rows // fields

    @pl.when(step == 0)
    def _():
        acc[...] = jnp.zeros_like(acc)

    lane = lax.broadcasted_iota(jnp.int32, (1, innov.shape[1]), 1)
    for i in range(blocks):
        block = step * blocks + i
        seen = (lane < count[block]).astype(jnp.float32).astype(jnp.bfloat16)
        masked = innov[i * rows : (i + 1) * rows, :] * seen
        product = jnp.dot(masked, oper[i], preferred_element_type=jnp.float32)
        spot = owner[block] * lats + block_row[block]
        product = product.astype(jnp.bfloat16).astype(jnp.float32)
        for half in range(acc.shape[1]):
            part = product[:, half * LANES : (half + 1) * LANES]
            acc[spot, half] = acc[spot, half] + part

    def by_field(spot, lev):
        halves = [
            acc[spot, half, pl.ds(lev, fields, stride=levs), :] for half in range(acc.shape[1])
        ]
        return jnp.concatenate(halves, axis=1)

    @pl.when(step == pl.num_programs(0) - 1)
    def _():
        if len(outs) == 2:
            mine = lax.axis_index("lon")
            for out, tile in zip(outs, (mine, 1 - mine)):
                for row in range(lats):
                    for lev in range(levs):
                        value = by_field(tile * lats + row, lev)
                        out[lev, row] = value.astype(out.dtype)
        else:
            (out,) = outs
            for tile in range(out.shape[0]):
                for row in range(lats):
                    for lev in range(levs):
                        out[tile, lev, row] = by_field(tile * lats + row, lev)


def lat_kernel(own, from_a, from_b, _, ext, to_a, to_b):
    levs, lats = own.shape[0], own.shape[1] - 1
    place = lax.axis_index("lat")
    even = lax.rem(place, 2) == 0
    south_in = (place > 0).astype(jnp.float32)
    north_in = (place < lax.axis_size("lat") - 1).astype(jnp.float32)
    south_wind, own_wind, north_wind = lats + 2 * STEPS, lats + 2 * STEPS + 1, lats + 2 * STEPS + 2

    def fill(south, north):
        for lev in range(levs):
            for row in range(STEPS):
                ext[lev, row] = south[lev, row].astype(jnp.float32) * south_in
                ext[lev, STEPS + lats + row] = north[lev, row].astype(jnp.float32) * north_in
            ext[lev, south_wind] = south[lev, STEPS].astype(jnp.float32)
            ext[lev, north_wind] = north[lev, STEPS].astype(jnp.float32)

    @pl.when(even)
    def _():
        fill(from_b, from_a)

    @pl.when(jnp.logical_not(even))
    def _():
        fill(from_a, from_b)

    for lev in range(levs):
        for row in range(lats):
            ext[lev, STEPS + row] = own[lev, row]
        ext[lev, own_wind] = own[lev, lats]
    odd = lax.rem(lax.axis_index("lev"), 2)
    sub = lax.broadcasted_iota(jnp.int32, own.shape[2:], 0)
    outer = lax.rem(sub, lats) >= lats // 2
    for out, down in ((to_a, odd), (to_b, 1 - odd)):
        at = 0
        for d, first, rows in lev_rows(lats):
            lev = down * (d - 1) + (1 - down) * (levs - d)
            for row in range(rows):
                out[at + row] = ext[lev, STEPS + first + row].astype(jnp.bfloat16)
            at += rows
        for d in range(1, STEPS):
            lev = down * (d - 1) + (1 - down) * (levs - d)
            out[at] = ext[lev, own_wind].astype(jnp.bfloat16)
            both = jnp.where(outer, ext[lev, south_wind], ext[lev, north_wind])
            out[at + 1] = both.astype(jnp.bfloat16)
            at += 2


def pack_order(levs, lats, lev_tiles):
    order = [("ext", lev, tile) for lev in range(levs) for tile in range(lats + 2 * STEPS + 3)]
    return order + [("lev", side, tile) for side in range(2) for tile in range(lev_tiles)]


def lev_kernel(ext, from_a, from_b, lev, edges):
    levs, lats = ext.shape[0], ext.shape[1] - 2 * STEPS - 3
    tiles = lev.shape[1]
    place = lax.axis_index("lev")
    even = lax.rem(place, 2) == 0
    below_in = (place > 0).astype(jnp.float32)
    above_in = (place < lax.axis_size("lev") - 1).astype(jnp.float32)

    def fill(below, above):
        for tile in range(tiles):
            lev[0, tile] = below[tile].astype(jnp.float32) * below_in
            lev[1, tile] = above[tile].astype(jnp.float32) * above_in

    @pl.when(even)
    def _():
        fill(from_b, from_a)

    @pl.when(jnp.logical_not(even))
    def _():
        fill(from_a, from_b)

    lane = lax.broadcasted_iota(jnp.int32, (ext.shape[2], LANES), 1)
    total = None
    order = pack_order(levs, lats, tiles)
    for n, (kind, i, tile) in enumerate(order):
        ref = ext if kind == "ext" else lev
        k = n % PER_TILE
        value = jnp.where(lane < GROUP, ref[i, tile, :, 0:LANES], ref[i, tile, :, -LANES:])
        value = pltpu.roll(value, GROUP * k + STEPS, 1)
        total = value if k == 0 else jnp.where(lane // GROUP == k, value, total)
        if k == PER_TILE - 1 or n == len(order) - 1:
            edges[n // PER_TILE] = total.astype(jnp.bfloat16)


def step_kernel(
    diff, vert, ext, lev, west, east, obs_a, obs_b, out_hbm, rows_a, rows_b, result, sem
):
    levs, lats = ext.shape[0], ext.shape[1] - 2 * STEPS - 3
    fields, lons = ext.shape[2], ext.shape[3]
    width = lons + LANES
    tiles = lev.shape[1]
    level_total = vert.shape[0]
    lat_place, lev_place = lax.axis_index("lat"), lax.axis_index("lev")
    south_in = (lat_place > 0).astype(jnp.float32)
    north_in = (lat_place < lax.axis_size("lat") - 1).astype(jnp.float32)
    below_in = (lev_place > 0).astype(jnp.float32)
    above_in = (lev_place < lax.axis_size("lev") - 1).astype(jnp.float32)
    where = {key: n for n, key in enumerate(pack_order(levs, lats, tiles))}
    lane = lax.broadcasted_iota(jnp.int32, (fields, LANES), 1)
    sub = lax.broadcasted_iota(jnp.int32, (fields, width), 0)
    hd = jnp.zeros((fields, width), jnp.float32)
    for f in range(fields):
        hd = jnp.where(sub == f, diff[f], hd)

    starts, at = {}, 0
    for d, first, rows in lev_rows(lats):
        starts[d] = (at, first)
        at += rows
    winds_at = at

    def source(k, j):
        if 0 <= k < levs:
            return ("ext", k, STEPS + j)
        side, d = (0, -k) if k < 0 else (1, k - levs + 1)
        begin, first = starts[d]
        return ("lev", side, begin + j - first)

    def wind_source(k, j, which):
        tile = 0 if j < 0 else (1 if j < lats else 2)
        row = which * lats + j % lats
        if 0 <= k < levs:
            return ("ext", k, lats + 2 * STEPS + tile), row
        side, d = (0, -k) if k < 0 else (1, k - levs + 1)
        return ("lev", side, winds_at + 2 * (d - 1) + (0 if tile == 1 else 1)), row

    opened = {}

    def edge(key):
        n = where[key]
        if n // PER_TILE not in opened:
            value_w = west[n // PER_TILE].astype(jnp.float32)
            opened[n // PER_TILE] = (
                (value_w, value_w)
                if west is east
                else (value_w, east[n // PER_TILE].astype(jnp.float32))
            )
        value_w, value_e = opened[n // PER_TILE]
        shift = (LANES - GROUP * (n % PER_TILE) - STEPS) % LANES
        if value_w is value_e:
            return pltpu.roll(value_w, shift, 1)
        return jnp.where(
            lane < LANES // 2, pltpu.roll(value_e, shift, 1), pltpu.roll(value_w, shift, 1)
        )

    def main(key):
        kind, i, tile = key
        return (ext if kind == "ext" else lev)[i, tile]

    def distance(k, j):
        dk = -k if k < 0 else max(0, k - levs + 1)
        dj = -j if j < 0 else max(0, j - lats + 1)
        return dk + dj

    def spot(k, j):
        return (k + STEPS) * (lats + 2 * STEPS) + j + STEPS

    cells = [(k, j) for k in range(-STEPS, levs + STEPS) for j in range(-STEPS, lats + STEPS)]
    for k, j in cells:
        if distance(k, j) <= STEPS:
            key = source(k, j)
            rows_a[spot(k, j), :, 0:lons] = main(key)
            rows_a[spot(k, j), :, lons:width] = edge(key)

    wind_edges = {}

    def wind(k, j, which):
        key, row = wind_source(k, j, which)
        if key not in wind_edges:
            wind_edges[key] = jnp.concatenate([main(key), edge(key)], axis=1)
        return wind_edges[key][row : row + 1, :]

    up, down = {}, {}
    for k in range(1 - STEPS, levs + STEPS - 1):
        level = lev_place * levs + k
        last = jnp.minimum(jnp.maximum(level, 0), level_total - 1)
        before = jnp.minimum(jnp.maximum(level - 1, 0), level_total - 1)
        up[k] = jnp.where(level < level_total - 1, vert[last], 0.0)
        down[k] = jnp.where(level >= 1, vert[before], 0.0)

    source_rows, target_rows = rows_a, rows_b
    copies = []
    for n in range(1, STEPS + 1):
        for k, j in cells:
            if distance(k, j) > STEPS - n:
                continue
            a = source_rows[spot(k, j)]
            u, w = wind(k, j, 0), wind(k, j, 1)
            north = source_rows[spot(k, j + 1)]
            east_part = (u + hd) * a
            new = a * (1.0 - up[k] - down[k] - u - w - 4.0 * hd)
            new = new + pltpu.roll(east_part, width - 1, 1) + hd * pltpu.roll(a, 1, 1)
            new = new + (wind(k, j + 1, 1) + hd) * north + hd * source_rows[spot(k, j - 1)]
            new = new + up[k] * source_rows[spot(k + 1, j)]
            new = new + down[k] * source_rows[spot(k - 1, j)]
            if k < 0:
                new = new * below_in
            elif k >= levs:
                new = new * above_in
            if j < 0:
                new = new * south_in
            elif j >= lats:
                new = new * north_in
            if n < STEPS:
                target_rows[spot(k, j)] = new
            else:
                obs = obs_a[k, j]
                if obs_b is not None:
                    obs = obs + obs_b[k, j].astype(jnp.float32)
                result[k, j] = new[:, 0:lons] + obs
        source_rows, target_rows = target_rows, source_rows
    for f in range(fields):
        copies.append(pltpu.make_async_copy(result.at[:, :, f, :], out_hbm.at[f], sem.at[f]))
        copies[-1].start()
    for copy in copies:
        copy.wait()


def on_device(
    adjoint_in,
    courant_lon,
    courant_lat,
    horiz_diff,
    vert_diff,
    innovations,
    obs_operator,
    owner_tile,
    block_row,
    obs_count,
):
    fields, levs, lats, lons = adjoint_in.shape
    blocks, _, _, obs_rows = innovations.shape
    n_lon, n_lat, n_lev = (lax.axis_size(axis) for axis in ("lon", "lat", "lev"))
    f32, bf16 = jnp.float32, jnp.bfloat16
    assert lats >= STEPS and levs >= STEPS and lons % LANES == 0 and fields == 2 * lats

    tile = (fields, lons)
    smalls = (owner_tile[:, 0], block_row, obs_count)
    inputs = (adjoint_in, courant_lon, courant_lat) + smalls
    own, to_lat_a, to_lat_b, *smalls = pl.pallas_call(
        load_kernel,
        out_shape=(
            jax.ShapeDtypeStruct((levs, lats + 1) + tile, f32),
            jax.ShapeDtypeStruct((levs, STEPS + 1) + tile, bf16),
            jax.ShapeDtypeStruct((levs, STEPS + 1) + tile, bf16),
        )
        + tuple(jax.ShapeDtypeStruct(x.shape, x.dtype) for x in smalls),
        in_specs=[HBM] * 6,
        out_specs=(VMEM,) * 6,
        scratch_shapes=[pltpu.SemaphoreType.DMA((fields + 5,))],
        cost_estimate=cost(1, 64 << 20),
        compiler_params=PARAMS,
        name="load",
    )(*(pltpu.with_memory_space_constraint(x, pltpu.HBM) for x in inputs))
    from_lat_a = lax.ppermute(to_lat_a, ("lat", "lev"), pair_up(n_lat, 0, n_lev, True))
    from_lat_b = lax.ppermute(to_lat_b, ("lat", "lev"), pair_up(n_lat, 1, n_lev, True))

    group = 8
    while blocks % group:
        group //= 2
    rows = fields * levs
    targets = n_lon * lats
    if n_lon == 2:
        obs_out = (
            jax.ShapeDtypeStruct((levs, lats) + tile, f32),
            jax.ShapeDtypeStruct((levs, lats) + tile, bf16),
        )
    else:
        obs_out = (jax.ShapeDtypeStruct((n_lon, levs, lats) + tile, f32),)
    obs = pl.pallas_call(
        functools.partial(obs_kernel, lats),
        out_shape=obs_out,
        grid_spec=pltpu.PrefetchScalarGridSpec(
            num_scalar_prefetch=3,
            grid=(blocks // group,),
            in_specs=[
                pl.BlockSpec((group * rows, obs_rows), lambda i, *_: (i, 0)),
                pl.BlockSpec((group, obs_rows, lons), lambda i, *_: (i, 0, 0)),
            ],
            out_specs=(VMEM,) * len(obs_out),
            scratch_shapes=[pltpu.VMEM((targets, lons // LANES, rows, LANES), f32)],
        ),
        cost_estimate=cost(2 * blocks * rows * obs_rows * lons, 12 << 20),
        compiler_params=PARAMS,
        name="obs",
    )(
        *smalls,
        innovations.reshape(blocks * rows, obs_rows),
        obs_operator,
    )

    lev_tiles = sum(rows for _, _, rows in lev_rows(lats)) + 2 * (STEPS - 1)
    ext_tiles = lats + 2 * STEPS + 3
    ext, to_lev_a, to_lev_b = pl.pallas_call(
        lat_kernel,
        out_shape=(
            jax.ShapeDtypeStruct((levs, ext_tiles) + tile, f32),
            jax.ShapeDtypeStruct((lev_tiles,) + tile, bf16),
            jax.ShapeDtypeStruct((lev_tiles,) + tile, bf16),
        ),
        in_specs=[VMEM] * 3 + [ANY],
        out_specs=(VMEM,) * 3,
        cost_estimate=cost(1, 1 << 20),
        compiler_params=PARAMS,
        name="extend_lat",
    )(own, from_lat_a, from_lat_b, obs[0])
    from_lev_b = lax.ppermute(to_lev_b, ("lat", "lev"), pair_up(n_lev, 1, n_lat, False))
    from_lev_a = lax.ppermute(to_lev_a, ("lat", "lev"), pair_up(n_lev, 0, n_lat, False))

    if n_lon == 2:
        obs_own = obs[0]
        obs_from = lax.ppermute(obs[1], "lon", [(0, 1), (1, 0)])
    else:
        flat = obs[0].reshape(-1, lons)
        obs_own = lax.psum_scatter(flat, "lon", scatter_dimension=0, tiled=True)
        obs_own = obs_own.reshape((levs, lats) + tile)
        obs_from = None

    packed = -(-(levs * ext_tiles + 2 * lev_tiles) // PER_TILE)
    lev, edges = pl.pallas_call(
        lev_kernel,
        out_shape=(
            jax.ShapeDtypeStruct((2, lev_tiles) + tile, f32),
            jax.ShapeDtypeStruct((packed, fields, LANES), bf16),
        ),
        in_specs=[VMEM] * 3,
        out_specs=(VMEM,) * 2,
        cost_estimate=cost(1, 1 << 20),
        compiler_params=PARAMS,
        name="extend_lev",
    )(ext, from_lev_a, from_lev_b)
    east_ring = [(i, (i + 1) % n_lon) for i in range(n_lon)]
    west = lax.ppermute(edges, "lon", east_ring)
    halos = [west]
    if n_lon > 2:
        halos.append(lax.ppermute(edges, "lon", [(b, a) for a, b in east_ring]))
    sums = [obs_own] if obs_from is None else [obs_own, obs_from]

    def run(diff, vert, ext_ref, lev_ref, *refs):
        halo_refs, rest = refs[: len(halos)], refs[len(halos) :]
        obs_refs, rest = rest[: len(sums)], rest[len(sums) :]
        step_kernel(
            diff,
            vert,
            ext_ref,
            lev_ref,
            halo_refs[0],
            halo_refs[-1],
            obs_refs[0],
            obs_refs[1] if len(sums) == 2 else None,
            *rest,
        )

    grid_rows = (levs + 2 * STEPS) * (lats + 2 * STEPS)
    return pl.pallas_call(
        run,
        out_shape=jax.ShapeDtypeStruct(adjoint_in.shape, f32),
        in_specs=[SMEM, SMEM] + [VMEM] * (2 + len(halos) + len(sums)),
        out_specs=ANY,
        scratch_shapes=[
            pltpu.VMEM((grid_rows, fields, lons + LANES), f32),
            pltpu.VMEM((grid_rows, fields, lons + LANES), f32),
            pltpu.VMEM((levs, lats) + tile, f32),
            pltpu.SemaphoreType.DMA((fields,)),
        ],
        cost_estimate=cost(1, 4 << 20),
        compiler_params=PARAMS,
        name="sub_steps",
    )(horiz_diff, vert_diff, ext, lev, *halos, *sums)


def solution(mesh):
    in_specs = (
        P(None, "lev", "lat", "lon"),
        P("lev", "lat", "lon"),
        P("lev", "lat", "lon"),
        P(),
        P(),
        P(("lon", "lat"), None, "lev", None),
        P(("lon", "lat"), None, None),
        P(("lon", "lat"), None),
        P(("lon", "lat")),
        P(("lon", "lat")),
    )
    out_specs = P(None, "lev", "lat", "lon")
    return jax.shard_map(
        on_device, mesh=mesh, in_specs=in_specs, out_specs=out_specs, check_vma=False
    )
```

time: 49.1 us -> 22.5 us (0.46)
  the two profiles are of different devices: /device:TPU:1 before, /device:TPU:0 now
where the time goes in v2:
time: 22.5 us; the launch traced here: 22.2 us
  starting transfers between devices  9.48 us (42%)
  Pallas kernels  6.09 us (27%)
  waiting for transfers between devices  3.37 us (15%)
  local copies, waits for them, and re-layouts  3.24 us (14%)
    unnamed x8, local copies, waits for them, and re-layouts  3.24 us
    ppermute x1, starting transfers between devices, on_device(): lax.ppermute(to_lat_a, ('lat', 'lev'), pair_up(n_lat, 0, n_lev, True))  3.14 us
    ppermute x1, starting transfers between devices, on_device(): lax.ppermute(to_lev_b, ('lat', 'lev'), pair_up(n_lev, 1, n_lat, False))  2.73 us
    pallas_call x1, Pallas kernels, on_device(): pl.pallas_call(run, out_shape=jax.ShapeDtypeStruct(adjoint_in.shape, f32)...  2.52 us
    pallas_call x1, Pallas kernels, on_device(): pl.pallas_call(functools.partial(obs_kernel, lats), out_shape=obs_out, gr...  2.36 us
    ppermute x1, waiting for transfers between devices, on_device(): west = lax.ppermute(edges, 'lon', east_ring)  2.14 us
    ppermute x1, starting transfers between devices, on_device(): west = lax.ppermute(edges, 'lon', east_ring)  1.55 us
    ppermute x1, starting transfers between devices, on_device(): obs_from = lax.ppermute(obs[1], 'lon', [(0, 1), (1, 0)])  1.48 us
  transfers between devices with their start and end apart: 6, of which 3 were waited for; matrix products, arithmetic and copies ran while one was open for 0% of the time, Pallas kernels for 11%

profile of v2, /device:TPU:0, one launch (start us, length us, event | category | flops | bytes accessed | tf_op | source)
XLA Modules:
  0.0 22.2 jit_solution(5365768613146932215)
XLA Ops:
  0.0 0.0 copy-start.3
  0.0 0.0 copy-start.2
  0.0 1.0 %load.1 = (f32[4,5,8,256]{3,2,1,0:T(8,128)S(1)}, bf16[4,4,8,256]{3,2,1,0:T(8,128)(2,1)S(1)}, bf16[4,4,8,256]{3,2,1,0:T(8,128)(2,1)S(1)}, s32[64]{0:T(128)S(1)}, s32[64]{0:T(128)S(1)}, /*index=5*/s32[64]{0:T(128)S(1)}) custom-call(f32[8,4,4,256]{3,2,1,0:T(4,128)} %adj.1, f32[4,4,256]{2,1,0:T(4,128)} %wind_u.1, f32[4,4,256]{2,1,0:T(4,128)} %wind_w.1, ...), custom_call_target="tpu_custom_call" | custom-call | flops 1 | bytes 67108864 | tf_op jit(solution)/shard_map/load/pallas_call | solution.py:353
  1.0 3.1 %collective-permute-start = (bf16[4,4,8,256]{3,2,1,0:T(8,128)(2,1)S(1)}, bf16[4,4,8,256]{3,2,1,0:T(8,128)(2,1)S(1)}, u32[]{:S(2)}, u32[]{:S(2)}) collective-permute-start(bf16[4,4,8,256]{3,2,1,0:T(8,128)(2,1)S(1)} %get-tuple-element.19), channel_id=1, source_target_pairs={{0,4},{1,5},{2,6},{3,7},{4,0},{5,1},{6,2},{7,3},{8,12},{9,13},{10,... | collective-permute-start | bytes 196616 | tf_op jit(solution)/shard_map/ppermute | solution.py:368
  4.2 0.0 collective-permute-start.1
  4.2 0.0 copy-start
  4.2 2.2 %copy-done = bf16[64,128,256]{2,1,0:T(8,128)(2,1)S(1)} copy-done((bf16[64,128,256]{2,1,0:T(8,128)(2,1)S(1)}, bf16[64,128,256]{2,1,0:T(8,128)(2,1)}, u32[]{:S(2)}) %copy-start) | copy-done | bytes 4194328
  6.3 1.0 %copy-done.1 = bf16[64,8,4,128]{3,2,1,0:T(4,128)(2,1)S(1)} copy-done((bf16[64,8,4,128]{3,2,1,0:T(4,128)(2,1)S(1)}, bf16[64,8,4,128]{3,2,1,0:T(4,128)(2,1)}, u32[]{:S(2)}) %copy-start.1) | copy-done | bytes 524312
  7.4 2.4 %obs.1 = (f32[4,4,8,256]{3,2,1,0:T(8,128)S(1)}, bf16[4,4,8,256]{3,2,1,0:T(8,128)(2,1)S(1)}) custom-call(s32[64]{0:T(128)S(1)} %get-tuple-element.21.owner, s32[64]{0:T(128)S(1)} %get-tuple-element.22.block_row, s32[64]{0:T(128)S(1)} %get-tuple-element.23.count, bf16[2048,128]{1,0:T(8,128)(2,1)S(1)} %bitcast.2, bf16[64,128,256]{2,1,0:T(8,128)(2,1)S(1)} %copy-done), custom_call_target="tpu_custom_call" | custom-call | flops 134217728 | bytes 12582912 | tf_op jit(solution)/shard_map/obs/pallas_call | solution.py:383
  9.8 0.0 collective-permute-done.from_a
  9.8 0.0 collective-permute-done.1.from_b
  9.8 0.1 extend_lat.1
  9.9 0.6 %collective-permute-start.2 = (bf16[22,8,256]{2,1,0:T(8,128)(2,1)S(1)}, bf16[22,8,256]{2,1,0:T(8,128)(2,1)S(1)}, u32[]{:S(2)}, u32[]{:S(2)}) collective-permute-start(bf16[22,8,256]{2,1,0:T(8,128)(2,1)S(1)} %get-tuple-element.26), channel_id=1, source_target_pairs={{0,1},{4,5},{8,9},{12,13},{1,0},{5,4},{9,8},{13,12},{2,3},{6,7},{1... | collective-permute-start | bytes 270344 | tf_op jit(solution)/shard_map/ppermute | solution.py:421
  10.4 2.7 %collective-permute-start.3 = (bf16[22,8,256]{2,1,0:T(8,128)(2,1)S(1)}, bf16[22,8,256]{2,1,0:T(8,128)(2,1)S(1)}, u32[]{:S(2)}, u32[]{:S(2)}) collective-permute-start(bf16[22,8,256]{2,1,0:T(8,128)(2,1)S(1)} %get-tuple-element.27), channel_id=1, source_target_pairs={{0,4},{4,0},{8,12},{12,8},{1,2},{5,6},{9,10},{13,14},{2,1},{6,5},{... | collective-permute-start | bytes 270344 | tf_op jit(solution)/shard_map/ppermute | solution.py:420
  13.2 1.5 %collective-permute-start.5 = (bf16[4,4,8,256]{3,2,1,0:T(8,128)(2,1)S(1)}, bf16[4,4,8,256]{3,2,1,0:T(8,128)(2,1)S(1)}, u32[]{:S(2)}, u32[]{:S(2)}) collective-permute-start(bf16[4,4,8,256]{3,2,1,0:T(8,128)(2,1)S(1)} %get-tuple-element.30), channel_id=1, source_target_pairs={{0,16},{16,0},{1,17},{17,1},{2,18},{18,2},{3,19},{19,3},{4,20},{20... | collective-permute-start | bytes 196616 | tf_op jit(solution)/shard_map/ppermute | solution.py:425
  14.6 0.0 collective-permute-done.2.from_a
  14.6 1.0 %collective-permute-done.3.from_b = bf16[22,8,256]{2,1,0:T(8,128)(2,1)S(1)} collective-permute-done((bf16[22,8,256]{2,1,0:T(8,128)(2,1)S(1)}, bf16[22,8,256]{2,1,0:T(8,128)(2,1)S(1)}, u32[]{:S(2)}, u32[]{:S(2)}) %collective-permute-start.3) | collective-permute-done | bytes 90144 | tf_op jit(solution)/shard_map/ppermute | solution.py:420
  15.7 0.1 extend_lev.1
  15.8 1.5 %collective-permute-start.4 = (bf16[12,8,128]{2,1,0:T(8,128)(2,1)S(1)}, bf16[12,8,128]{2,1,0:T(8,128)(2,1)S(1)}, u32[]{:S(2)}, u32[]{:S(2)}) collective-permute-start(bf16[12,8,128]{2,1,0:T(8,128)(2,1)S(1)} %get-tuple-element.29), channel_id=1, source_target_pairs={{0,16},{16,0},{1,17},{17,1},{2,18},{18,2},{3,19},{19,3},{4,20},{20... | collective-permute-start | bytes 73736 | tf_op jit(solution)/shard_map/ppermute | solution.py:446
  17.4 0.2 collective-permute-done.5.refs_2_
  17.6 2.1 %collective-permute-done.4.refs_0_ = bf16[12,8,128]{2,1,0:T(8,128)(2,1)S(1)} collective-permute-done((bf16[12,8,128]{2,1,0:T(8,128)(2,1)S(1)}, bf16[12,8,128]{2,1,0:T(8,128)(2,1)S(1)}, u32[]{:S(2)}, u32[]{:S(2)}) %collective-permute-start.4) | collective-permute-done | bytes 24608 | tf_op jit(solution)/shard_map/ppermute | solution.py:446
  19.7 0.0 copy-done.3
  19.7 0.0 copy-done.2
  19.7 2.5 %sub_steps.1 = f32[8,4,4,256]{3,2,1,0:T(4,128)} custom-call(f32[8]{0:T(128)S(1)} %copy-done.2, f32[16]{0:T(128)S(1)} %copy-done.3, f32[4,13,8,256]{3,2,1,0:T(8,128)S(1)} %get-tuple-element.25.ext.ext_ref, f32[2,22,8,256]{3,2,1,0:T(8,128)S(1)} %get-tuple-element.28.lev_ref, bf16[12,8,128]{2,1,0:T(8,128)(2,1)S(1)} %collective-permute-done.4.refs_0_, ...), custom_call_target="tpu_custom_call" | custom-call | flops 1 | bytes 4194304 | tf_op jit(solution)/shard_map/sub_steps/pallas_call | solution.py:468
  (1 shorter events, 0.0 us)
Async XLA Ops:
  0.0 19.7 %copy-start.3 = (f32[16]{0:T(128)S(1)}, f32[16]{0:T(128)}, u32[]{:S(2)}) copy-start(f32[16]{0:T(128)} %vert.1) | copy-start | bytes 196
  0.0 19.7 %copy-start.2 = (f32[8]{0:T(128)S(1)}, f32[8]{0:T(128)}, u32[]{:S(2)}) copy-start(f32[8]{0:T(128)} %diff.1) | copy-start | bytes 100
  1.0 8.7 %collective-permute-start = (bf16[4,4,8,256]{3,2,1,0:T(8,128)(2,1)S(1)}, bf16[4,4,8,256]{3,2,1,0:T(8,128)(2,1)S(1)}, u32[]{:S(2)}, u32[]{:S(2)}) collective-permute-start(bf16[4,4,8,256]{3,2,1,0:T(8,128)(2,1)S(1)} %get-tuple-element.19), channel_id=1, source_target_pairs={{0,4},{1,5},{2,6},{3,7},{4,0},{5,1},{6,2},{7,3},{8,12},{9,13},{10,... | collective-permute-start | bytes 196616 | tf_op jit(solution)/shard_map/ppermute | solution.py:368
  4.2 5.6 %collective-permute-start.1 = (bf16[4,4,8,256]{3,2,1,0:T(8,128)(2,1)S(1)}, bf16[4,4,8,256]{3,2,1,0:T(8,128)(2,1)S(1)}, u32[]{:S(2)}, u32[]{:S(2)}) collective-permute-start(bf16[4,4,8,256]{3,2,1,0:T(8,128)(2,1)S(1)} %get-tuple-element.20), channel_id=1, source_target_pairs={{0,1},{1,0},{2,3},{3,2},{4,8},{5,9},{6,10},{7,11},{8,4},{9,5},{10,... | collective-permute-start | bytes 196616 | tf_op jit(solution)/shard_map/ppermute | solution.py:369
  4.2 2.2 %copy-start = (bf16[64,128,256]{2,1,0:T(8,128)(2,1)S(1)}, bf16[64,128,256]{2,1,0:T(8,128)(2,1)}, u32[]{:S(2)}) copy-start(bf16[64,128,256]{2,1,0:T(8,128)(2,1)} %oper.1) | copy-start | bytes 12582916
  6.3 1.0 %copy-start.1 = (bf16[64,8,4,128]{3,2,1,0:T(4,128)(2,1)S(1)}, bf16[64,8,4,128]{3,2,1,0:T(4,128)(2,1)}, u32[]{:S(2)}) copy-start(bf16[64,8,4,128]{3,2,1,0:T(4,128)(2,1)} %param.15) | copy-start | bytes 1572868
  9.9 4.8 %collective-permute-start.2 = (bf16[22,8,256]{2,1,0:T(8,128)(2,1)S(1)}, bf16[22,8,256]{2,1,0:T(8,128)(2,1)S(1)}, u32[]{:S(2)}, u32[]{:S(2)}) collective-permute-start(bf16[22,8,256]{2,1,0:T(8,128)(2,1)S(1)} %get-tuple-element.26), channel_id=1, source_target_pairs={{0,1},{4,5},{8,9},{12,13},{1,0},{5,4},{9,8},{13,12},{2,3},{6,7},{1... | collective-permute-start | bytes 270344 | tf_op jit(solution)/shard_map/ppermute | solution.py:421
  10.4 5.2 %collective-permute-start.3 = (bf16[22,8,256]{2,1,0:T(8,128)(2,1)S(1)}, bf16[22,8,256]{2,1,0:T(8,128)(2,1)S(1)}, u32[]{:S(2)}, u32[]{:S(2)}) collective-permute-start(bf16[22,8,256]{2,1,0:T(8,128)(2,1)S(1)} %get-tuple-element.27), channel_id=1, source_target_pairs={{0,4},{4,0},{8,12},{12,8},{1,2},{5,6},{9,10},{13,14},{2,1},{6,5},{... | collective-permute-start | bytes 270344 | tf_op jit(solution)/shard_map/ppermute | solution.py:420
  13.2 4.4 %collective-permute-start.5 = (bf16[4,4,8,256]{3,2,1,0:T(8,128)(2,1)S(1)}, bf16[4,4,8,256]{3,2,1,0:T(8,128)(2,1)S(1)}, u32[]{:S(2)}, u32[]{:S(2)}) collective-permute-start(bf16[4,4,8,256]{3,2,1,0:T(8,128)(2,1)S(1)} %get-tuple-element.30), channel_id=1, source_target_pairs={{0,16},{16,0},{1,17},{17,1},{2,18},{18,2},{3,19},{19,3},{4,20},{20... | collective-permute-start | bytes 196616 | tf_op jit(solution)/shard_map/ppermute | solution.py:425
  15.8 3.9 %collective-permute-start.4 = (bf16[12,8,128]{2,1,0:T(8,128)(2,1)S(1)}, bf16[12,8,128]{2,1,0:T(8,128)(2,1)S(1)}, u32[]{:S(2)}, u32[]{:S(2)}) collective-permute-start(bf16[12,8,128]{2,1,0:T(8,128)(2,1)S(1)} %get-tuple-element.29), channel_id=1, source_target_pairs={{0,16},{16,0},{1,17},{17,1},{2,18},{18,2},{3,19},{19,3},{4,20},{20... | collective-permute-start | bytes 73736 | tf_op jit(solution)/shard_map/ppermute | solution.py:446

commit v3 on v2

v3 whole, which is shorter than its diff:
```python
import functools

import jax
import jax.numpy as jnp
from jax import lax
from jax.experimental import pallas as pl
from jax.experimental.pallas import tpu as pltpu
from jax.sharding import PartitionSpec as P

STEPS = 3
LANES = 128
GROUP = 16
PER_TILE = LANES // GROUP
VMEM = pl.BlockSpec(memory_space=pltpu.VMEM)
SMEM = pl.BlockSpec(memory_space=pltpu.SMEM)
ANY = pl.BlockSpec(memory_space=pl.ANY)
HBM = pl.BlockSpec(memory_space=pltpu.HBM)


PARAMS = pltpu.CompilerParams(vmem_limit_bytes=12 << 20)


def cost(flops, nbytes):
    return pl.CostEstimate(flops=flops, bytes_accessed=nbytes, transcendentals=0)


def pair_up(sizes, axis, phase, shift=0):
    n_lon, n_lat, n_lev = sizes
    pairs = []
    for lon in range(n_lon):
        for lat in range(n_lat):
            for lev in range(n_lev):
                to = [(lon + shift) % n_lon, lat, lev]
                if axis:
                    mate = to[axis] + (1 if to[axis] % 2 == phase else -1)
                    if 0 <= mate < sizes[axis]:
                        to[axis] = mate
                    elif shift % n_lon == 0:
                        to[3 - axis] ^= 1
                        if to[3 - axis] >= sizes[3 - axis]:
                            continue
                ends = [(p * n_lat + q) * n_lev + r for p, q, r in ((lon, lat, lev), to)]
                pairs.append(tuple(ends))
    return pairs


def send(x, pairs):
    return lax.ppermute(x, ("lon", "lat", "lev"), pairs)


def pack(tiles, out, at):
    total = None
    for n, value in enumerate(tiles):
        k = n % PER_TILE
        lane = lax.broadcasted_iota(jnp.int32, (value.shape[0], LANES), 1)
        value = jnp.where(lane < LANES // 2, value[:, 0:LANES], value[:, -LANES:])
        if k:
            value = pltpu.roll(value, GROUP * k, 1)
            value = jnp.where((lane + STEPS) % LANES // GROUP == k, value, total)
        total = value
        if k == PER_TILE - 1 or n == len(tiles) - 1:
            total = jnp.where(lane % GROUP < GROUP // 2, total, pltpu.roll(total, GROUP, 1))
            out[at + n // PER_TILE] = total.astype(out.dtype)


def lev_rows(lat_cells):
    return [(d, -(STEPS - d), lat_cells + 2 * (STEPS - d)) for d in range(1, STEPS + 1)]


def load_kernel(adj, wind_u, wind_w, *refs):
    small, (own, to_a, to_b), small_out, sem = refs[:3], refs[3:6], refs[6:9], refs[9]
    fields, levs, lats = adj.shape[:3]
    copies = [
        pltpu.make_async_copy(adj.at[f], own.at[:, 0:lats, f, :], sem.at[f]) for f in range(fields)
    ]
    copies.append(pltpu.make_async_copy(wind_u, own.at[:, lats, 0:lats, :], sem.at[fields]))
    copies.append(
        pltpu.make_async_copy(wind_w, own.at[:, lats, lats : 2 * lats, :], sem.at[fields + 1])
    )
    for n, (source, target) in enumerate(zip(small, small_out)):
        copies.append(pltpu.make_async_copy(source, target, sem.at[fields + 2 + n]))
    for copy in copies:
        copy.start()
    for copy in copies:
        copy.wait()
    odd = lax.rem(lax.axis_index("lat"), 2)
    for out, start in ((to_a, (1 - odd) * (lats - STEPS)), (to_b, odd * (lats - STEPS))):
        for lev in range(levs):
            for row in range(STEPS):
                out[lev, row] = own[lev, start + row].astype(jnp.bfloat16)
            out[lev, STEPS] = own[lev, lats].astype(jnp.bfloat16)


def obs_kernel(lats, owner, block_row, count, innov, oper, *refs):
    outs, (lhs, rhs, acc, sem) = refs[:-4], refs[-4:]
    blocks = oper.shape[0]
    rows = innov.shape[0] // blocks
    fields = 2 * lats
    levs = rows // fields
    chunks = sem.shape[1]
    per = blocks // chunks
    copies = []
    for n in range(chunks):
        some, some_rows = pl.ds(n * per, per), pl.ds(n * per * rows, per * rows)
        copies.append(
            (
                pltpu.make_async_copy(innov.at[some_rows], lhs.at[some_rows], sem.at[0, n]),
                pltpu.make_async_copy(oper.at[some], rhs.at[some], sem.at[1, n]),
            )
        )
        for copy in copies[-1]:
            copy.start()
    acc[...] = jnp.zeros_like(acc)
    lane = lax.broadcasted_iota(jnp.int32, (1, innov.shape[1]), 1)
    for block in range(blocks):
        if block % per == 0:
            for copy in copies[block // per]:
                copy.wait()
        seen = (lane < count[block]).astype(jnp.float32).astype(jnp.bfloat16)
        masked = lhs[block * rows : (block + 1) * rows, :] * seen
        product = jnp.dot(masked, rhs[block], preferred_element_type=jnp.float32)
        spot = owner[block] * lats + block_row[block]
        product = product.astype(jnp.bfloat16).astype(jnp.float32)
        for half in range(acc.shape[1]):
            part = product[:, half * LANES : (half + 1) * LANES]
            acc[spot, half] = acc[spot, half] + part

    def by_field(spot, lev):
        halves = [
            acc[spot, half, pl.ds(lev, fields, stride=levs), :] for half in range(acc.shape[1])
        ]
        return jnp.concatenate(halves, axis=1)

    if len(outs) == 2:
        mine = lax.axis_index("lon")
        for out, tile in zip(outs, (mine, 1 - mine)):
            for row in range(lats):
                for lev in range(levs):
                    out[lev, row] = by_field(tile * lats + row, lev).astype(out.dtype)
    else:
        (out,) = outs
        for tile in range(out.shape[0]):
            for row in range(lats):
                for lev in range(levs):
                    out[tile, lev, row] = by_field(tile * lats + row, lev)


def lat_kernel(own, from_a, from_b, obs, ext, to_a, to_b, edges, edges_a, edges_b):
    levs, lats = own.shape[0], own.shape[1] - 1
    place = lax.axis_index("lat")
    even = lax.rem(place, 2) == 0
    south_in = (place > 0).astype(jnp.float32)
    north_in = (place < lax.axis_size("lat") - 1).astype(jnp.float32)
    south_wind, own_wind, north_wind = lats + 2 * STEPS, lats + 2 * STEPS + 1, lats + 2 * STEPS + 2

    def fill(south, north):
        for lev in range(levs):
            for row in range(STEPS):
                ext[lev, row] = south[lev, row].astype(jnp.float32) * south_in
                ext[lev, STEPS + lats + row] = north[lev, row].astype(jnp.float32) * north_in
            ext[lev, south_wind] = south[lev, STEPS].astype(jnp.float32)
            ext[lev, north_wind] = north[lev, STEPS].astype(jnp.float32)

    @pl.when(even)
    def _():
        fill(from_b, from_a)

    @pl.when(jnp.logical_not(even))
    def _():
        fill(from_a, from_b)

    for lev in range(levs):
        for row in range(lats):
            ext[lev, STEPS + row] = own[lev, row]
        ext[lev, own_wind] = own[lev, lats]
    odd = lax.rem(lax.axis_index("lev"), 2)
    sub = lax.broadcasted_iota(jnp.int32, own.shape[2:], 0)
    outer = lax.rem(sub, lats) >= lats // 2
    for out, packed, down in ((to_a, edges_a, odd), (to_b, edges_b, 1 - odd)):
        tiles = []
        for d, first, rows in lev_rows(lats):
            lev = down * (d - 1) + (1 - down) * (levs - d)
            tiles += [ext[lev, STEPS + first + row] for row in range(rows)]
        for d in range(1, STEPS):
            lev = down * (d - 1) + (1 - down) * (levs - d)
            tiles.append(ext[lev, own_wind])
            tiles.append(jnp.where(outer, ext[lev, south_wind], ext[lev, north_wind]))
        for n, value in enumerate(tiles):
            out[n] = value.astype(jnp.bfloat16)
        pack(tiles, packed, 0)
    at = 0
    if edges.shape[0] > -(-levs * ext.shape[1] // PER_TILE):
        for lev in range(levs):
            for row in range(lats):
                for half in range(ext.shape[3] // LANES):
                    edges[at] = obs[lev, row, :, half * LANES : (half + 1) * LANES]
                    at += 1
    pack([ext[lev, n] for lev in range(levs) for n in range(ext.shape[1])], edges, at)


class Steps:
    def __init__(self, levs, lats, lev_tiles, level_total):
        self.levs, self.lats, self.level_total = levs, lats, level_total
        keys = [("ext", k, tile) for k in range(levs) for tile in range(lats + 2 * STEPS + 3)]
        keys += [("lev", side, tile) for side in range(2) for tile in range(lev_tiles)]
        self.order = {key: n for n, key in enumerate(keys)}
        self.starts, at = {}, 0
        for d, first, rows in lev_rows(lats):
            self.starts[d] = at - first
            at += rows
        self.winds_at = at
        self.cells = [
            (k, j) for k in range(-STEPS, levs + STEPS) for j in range(-STEPS, lats + STEPS)
        ]

    def distance(self, k, j):
        return max(-k, 0, k - self.levs + 1) + max(-j, 0, j - self.lats + 1)

    def spot(self, k, j):
        return (k + STEPS) * (self.lats + 2 * STEPS) + j + STEPS

    def side(self, k):
        return (0, -k) if k < 0 else (1, k - self.levs + 1)

    def source(self, k, j):
        if 0 <= k < self.levs:
            return ("ext", k, STEPS + j)
        side, d = self.side(k)
        return ("lev", side, self.starts[d] + j)

    def wind_source(self, k, j, which):
        tile = 0 if j < 0 else (1 if j < self.lats else 2)
        row = which * self.lats + j % self.lats
        if 0 <= k < self.levs:
            return ("ext", k, self.lats + 2 * STEPS + tile), row
        side, d = self.side(k)
        return ("lev", side, self.winds_at + 2 * (d - 1) + (0 if tile == 1 else 1)), row

    def run(self, diff, vert, shape, first_rows, wind, buffers, emit):
        levs, lats = self.levs, self.lats
        width = shape[1]
        lat_place, lev_place = lax.axis_index("lat"), lax.axis_index("lev")
        south_in = (lat_place > 0).astype(jnp.float32)
        north_in = (lat_place < lax.axis_size("lat") - 1).astype(jnp.float32)
        below_in = (lev_place > 0).astype(jnp.float32)
        above_in = (lev_place < lax.axis_size("lev") - 1).astype(jnp.float32)
        sub = lax.broadcasted_iota(jnp.int32, shape, 0)
        hd = jnp.zeros(shape, jnp.float32)
        for f in range(shape[0]):
            hd = jnp.where(sub == f, diff[f], hd)
        up, down = {}, {}
        for k in range(1 - STEPS, levs + STEPS - 1):
            level = lev_place * levs + k
            last = jnp.minimum(jnp.maximum(level, 0), self.level_total - 1)
            before = jnp.minimum(jnp.maximum(level - 1, 0), self.level_total - 1)
            up[k] = jnp.where(level < self.level_total - 1, vert[last], 0.0)
            down[k] = jnp.where(level >= 1, vert[before], 0.0)
        rows = first_rows
        for n in range(1, STEPS + 1):
            target = None if n == STEPS else buffers[(n - 1) % 2]
            for k, j in self.cells:
                if self.distance(k, j) > STEPS - n:
                    continue
                a = rows(k, j)
                u, w = wind(k, j, 0), wind(k, j, 1)
                new = a * (1.0 - up[k] - down[k] - u - w - 4.0 * hd)
                new = new + pltpu.roll((u + hd) * a, width - 1, 1) + hd * pltpu.roll(a, 1, 1)
                new = new + (wind(k, j + 1, 1) + hd) * rows(k, j + 1) + hd * rows(k, j - 1)
                new = new + up[k] * rows(k + 1, j) + down[k] * rows(k - 1, j)
                if k < 0:
                    new = new * below_in
                elif k >= levs:
                    new = new * above_in
                if j < 0:
                    new = new * south_in
                elif j >= lats:
                    new = new * north_in
                if target is None:
                    emit(k, j, new)
                else:
                    target[self.spot(k, j)] = new
            if target is not None:
                rows = functools.partial(lambda ref, k, j: ref[self.spot(k, j)], target)


EAST_END = LANES // 2
FIRST_AT = EAST_END + GROUP


def sides(low, high):
    place = lax.axis_index("lev")
    even = lax.rem(place, 2) == 0
    below_in = (place > 0).astype(jnp.float32)
    above_in = (place < lax.axis_size("lev") - 1).astype(jnp.float32)
    below, above = jnp.where(even, high, low), jnp.where(even, low, high)
    return below * below_in, above * above_in


def main_kernel(diff, vert, ext, from_a, from_b, result, edge_rows, lev, rows_a, rows_b):
    levs, lats = ext.shape[0], ext.shape[1] - 2 * STEPS - 3
    for tile in range(lev.shape[1]):
        low, high = from_a[tile].astype(jnp.float32), from_b[tile].astype(jnp.float32)
        lev[0, tile], lev[1, tile] = sides(low, high)
    steps = Steps(levs, lats, lev.shape[1], vert.shape[0])
    refs = {"ext": ext, "lev": lev}

    def first_rows(k, j):
        kind, i, tile = steps.source(k, j)
        return refs[kind][i, tile]

    def wind(k, j, which):
        (kind, i, tile), row = steps.wind_source(k, j, which)
        return refs[kind][i, tile, row : row + 1, :]

    def emit(k, j, new):
        result[k, j] = new

    steps.run(diff, vert, ext.shape[2:], first_rows, wind, (rows_a, rows_b), emit)
    lane = lax.broadcasted_iota(jnp.int32, edge_rows.shape[1:], 1)
    for n, (kind, i, tile) in enumerate(steps.order):
        first = pltpu.roll(refs[kind][i, tile, :, 0:LANES], FIRST_AT, 1)
        last = pltpu.roll(refs[kind][i, tile, :, -LANES:], EAST_END, 1)
        edge_rows[n] = jnp.where(lane < EAST_END, last, first)


def edge_kernel(levs, lats, lev_tiles, n_ways, diff, vert, main, own_rows, obs, *refs):
    halos, (out, edge_rows, rows_a, rows_b, result, sem) = refs[: 3 * n_ways], refs[3 * n_ways :]
    fields, lons = main.shape[2:]
    parts = lons // LANES
    steps = Steps(levs, lats, lev_tiles, vert.shape[0])
    lane = lax.broadcasted_iota(jnp.int32, (fields, LANES), 1)
    in_halo = (lane >= EAST_END) & (lane < FIRST_AT)
    ext_rows = len(steps.order) - 2 * lev_tiles
    obs_at = levs * lats * parts if n_ways == 1 else 0

    def packed(which, n):
        tiles = [halos[3 * way + which][n].astype(jnp.float32) for way in range(n_ways)]
        return jnp.where(lane % GROUP < GROUP // 2, tiles[-1], tiles[0])

    def unpack(tile, at, count):
        for k in range(count):
            halo = pltpu.roll(tile, (EAST_END - GROUP * k) % LANES, 1)
            edge_rows[at + k] = jnp.where(in_halo, halo, own_rows[at + k])

    for at in range(0, ext_rows, PER_TILE):
        unpack(packed(0, obs_at + at // PER_TILE), at, min(PER_TILE, ext_rows - at))
    for at in range(0, lev_tiles, PER_TILE):
        both = sides(packed(1, at // PER_TILE), packed(2, at // PER_TILE))
        for side, tile in enumerate(both):
            start = ext_rows + side * lev_tiles + at
            unpack(tile, start, min(PER_TILE, lev_tiles - at))

    def first_rows(k, j):
        return edge_rows[steps.order[steps.source(k, j)]]

    def wind(k, j, which):
        key, row = steps.wind_source(k, j, which)
        return edge_rows[steps.order[key], row : row + 1, :]

    def total(k, j, part):
        value = obs[k, j, :, part * LANES : (part + 1) * LANES]
        if n_ways == 1:
            value = value + halos[0][(k * lats + j) * parts + part].astype(jnp.float32)
        return value

    def emit(k, j, new):
        first = pltpu.roll(new, LANES - FIRST_AT, 1)
        last = pltpu.roll(new, LANES - EAST_END, 1)
        for part in range(parts):
            value = main[k, j, :, part * LANES : (part + 1) * LANES]
            if part == 0:
                value = jnp.where(lane < STEPS, first, value)
            if part == parts - 1:
                value = jnp.where(lane >= LANES - STEPS, last, value)
            result[k, j, :, part * LANES : (part + 1) * LANES] = value + total(k, j, part)

    steps.run(diff, vert, (fields, LANES), first_rows, wind, (rows_a, rows_b), emit)
    copies = [
        pltpu.make_async_copy(result.at[:, :, f, :], out.at[f], sem.at[f]) for f in range(fields)
    ]
    for copy in copies:
        copy.start()
    for copy in copies:
        copy.wait()


def on_device(
    adjoint_in,
    courant_lon,
    courant_lat,
    horiz_diff,
    vert_diff,
    innovations,
    obs_operator,
    owner_tile,
    block_row,
    obs_count,
):
    fields, levs, lats, lons = adjoint_in.shape
    blocks, _, _, obs_rows = innovations.shape
    n_lon, n_lat, n_lev = (lax.axis_size(axis) for axis in ("lon", "lat", "lev"))
    f32, bf16 = jnp.float32, jnp.bfloat16
    assert lats >= STEPS and levs >= STEPS and lons % LANES == 0 and fields == 2 * lats

    tile = (fields, lons)
    smalls = (owner_tile[:, 0], block_row, obs_count)
    inputs = (adjoint_in, courant_lon, courant_lat) + smalls
    own, to_lat_a, to_lat_b, *smalls = pl.pallas_call(
        load_kernel,
        out_shape=(
            jax.ShapeDtypeStruct((levs, lats + 1) + tile, f32),
            jax.ShapeDtypeStruct((levs, STEPS + 1) + tile, bf16),
            jax.ShapeDtypeStruct((levs, STEPS + 1) + tile, bf16),
        )
        + tuple(jax.ShapeDtypeStruct(x.shape, x.dtype) for x in smalls),
        in_specs=[HBM] * 6,
        out_specs=(VMEM,) * 6,
        scratch_shapes=[pltpu.SemaphoreType.DMA((fields + 5,))],
        cost_estimate=cost(1, 64 << 20),
        compiler_params=PARAMS,
        name="load",
    )(*(pltpu.with_memory_space_constraint(x, pltpu.HBM) for x in inputs))
    sizes = (n_lon, n_lat, n_lev)
    from_lat_a = send(to_lat_a, pair_up(sizes, 1, 0))
    from_lat_b = send(to_lat_b, pair_up(sizes, 1, 1))

    chunks = 8
    while blocks % chunks:
        chunks //= 2
    rows = fields * levs
    targets = n_lon * lats
    if n_lon == 2:
        obs_out = (
            jax.ShapeDtypeStruct((levs, lats) + tile, f32),
            jax.ShapeDtypeStruct((levs, lats) + tile, bf16),
        )
    else:
        obs_out = (jax.ShapeDtypeStruct((n_lon, levs, lats) + tile, f32),)
    obs = pl.pallas_call(
        functools.partial(obs_kernel, lats),
        out_shape=obs_out,
        in_specs=[SMEM] * 3 + [HBM] * 2,
        out_specs=(VMEM,) * len(obs_out),
        scratch_shapes=[
            pltpu.VMEM((blocks * rows, obs_rows), bf16),
            pltpu.VMEM(obs_operator.shape, bf16),
            pltpu.VMEM((targets, lons // LANES, rows, LANES), f32),
            pltpu.SemaphoreType.DMA((2, chunks)),
        ],
        cost_estimate=cost(2 * blocks * rows * obs_rows * lons, 12 << 20),
        compiler_params=PARAMS,
        name="obs",
    )(
        *smalls,
        pltpu.with_memory_space_constraint(
            innovations.reshape(blocks * rows, obs_rows), pltpu.HBM
        ),
        pltpu.with_memory_space_constraint(obs_operator, pltpu.HBM),
    )

    lev_tiles = sum(rows for _, _, rows in lev_rows(lats)) + 2 * (STEPS - 1)
    ext_tiles = lats + 2 * STEPS + 3
    ext_packed, lev_packed = -(-levs * ext_tiles // PER_TILE), -(-lev_tiles // PER_TILE)
    obs_tiles = levs * lats * (lons // LANES) if n_lon == 2 else 0
    lane_tile = (fields, LANES)
    ext, to_lev_a, to_lev_b, edges, edges_a, edges_b = pl.pallas_call(
        lat_kernel,
        out_shape=(
            jax.ShapeDtypeStruct((levs, ext_tiles) + tile, f32),
            jax.ShapeDtypeStruct((lev_tiles,) + tile, bf16),
            jax.ShapeDtypeStruct((lev_tiles,) + tile, bf16),
            jax.ShapeDtypeStruct((obs_tiles + ext_packed,) + lane_tile, bf16),
            jax.ShapeDtypeStruct((lev_packed,) + lane_tile, bf16),
            jax.ShapeDtypeStruct((lev_packed,) + lane_tile, bf16),
        ),
        in_specs=[VMEM] * 4,
        out_specs=(VMEM,) * 6,
        cost_estimate=cost(1, 1 << 20),
        compiler_params=PARAMS,
        name="extend_lat",
    )(own, from_lat_a, from_lat_b, obs[-1])
    from_lev_b = send(to_lev_b, pair_up(sizes, 2, 1))
    from_lev_a = send(to_lev_a, pair_up(sizes, 2, 0))
    ways = (1,) if n_lon == 2 else (1, -1)
    halos = []
    for way in ways:
        halos.append(send(edges, pair_up(sizes, 0, 0, way)))
        halos.append(send(edges_a, pair_up(sizes, 2, 0, way)))
        halos.append(send(edges_b, pair_up(sizes, 2, 1, way)))
    if n_lon == 2:
        obs_own = obs[0]
    else:
        flat = obs[0].reshape(-1, lons)
        obs_own = lax.psum_scatter(flat, "lon", scatter_dimension=0, tiled=True)
        obs_own = obs_own.reshape((levs, lats) + tile)

    grid_rows = (levs + 2 * STEPS) * (lats + 2 * STEPS)
    edge_shape = (levs * ext_tiles + 2 * lev_tiles,) + lane_tile
    main, edge_rows = pl.pallas_call(
        main_kernel,
        out_shape=(
            jax.ShapeDtypeStruct((levs, lats) + tile, f32),
            jax.ShapeDtypeStruct(edge_shape, f32),
        ),
        in_specs=[SMEM] * 2 + [VMEM] * 3,
        out_specs=(VMEM,) * 2,
        scratch_shapes=[pltpu.VMEM((2, lev_tiles) + tile, f32)]
        + [pltpu.VMEM((grid_rows,) + tile, f32)] * 2,
        cost_estimate=cost(1, 8 << 20),
        compiler_params=PARAMS,
        name="sub_steps",
    )(horiz_diff, vert_diff, ext, from_lev_a, from_lev_b)
    return pl.pallas_call(
        functools.partial(edge_kernel, levs, lats, lev_tiles, len(ways)),
        out_shape=jax.ShapeDtypeStruct(adjoint_in.shape, f32),
        in_specs=[SMEM] * 2 + [VMEM] * (3 + len(halos)),
        out_specs=ANY,
        scratch_shapes=[
            pltpu.VMEM(edge_shape, f32),
            pltpu.VMEM((grid_rows, fields, LANES), f32),
            pltpu.VMEM((grid_rows, fields, LANES), f32),
            pltpu.VMEM((levs, lats) + tile, f32),
            pltpu.SemaphoreType.DMA((fields,)),
        ],
        cost_estimate=cost(1, 1 << 20),
        compiler_params=PARAMS,
        name="edges",
    )(horiz_diff, vert_diff, main, edge_rows, obs_own, *halos)


def solution(mesh):
    in_specs = (
        P(None, "lev", "lat", "lon"),
        P("lev", "lat", "lon"),
        P("lev", "lat", "lon"),
        P(),
        P(),
        P(("lon", "lat"), None, "lev", None),
        P(("lon", "lat"), None, None),
        P(("lon", "lat"), None),
        P(("lon", "lat")),
        P(("lon", "lat")),
    )
    out_specs = P(None, "lev", "lat", "lon")
    return jax.shard_map(
        on_device, mesh=mesh, in_specs=in_specs, out_specs=out_specs, check_vma=False
    )
```

time: 22.5 us -> 19 us (0.84)
  the two profiles are of different devices: /device:TPU:0 before, /device:TPU:1 now
where the time goes in v3:
time: 19 us; the launch traced here: 18.8 us
  starting transfers between devices  9.96 us (52%)
  Pallas kernels  8.23 us (43%)
  waiting for transfers between devices  0.51 us (3%)
    ppermute x7, starting transfers between devices, send(): return lax.ppermute(x, ('lon', 'lat', 'lev'), pairs)  9.96 us
    pallas_call x1, Pallas kernels, on_device(): pl.pallas_call(functools.partial(obs_kernel, lats), out_shape=obs_out, in...  3.49 us
    pallas_call x1, Pallas kernels, on_device(): pl.pallas_call(functools.partial(edge_kernel, levs, lats, lev_tiles, len(...  1.78 us
    pallas_call x1, Pallas kernels, on_device(): pl.pallas_call(main_kernel, out_shape=(jax.ShapeDtypeStruct((levs, lats)...  1.48 us
    pallas_call x1, Pallas kernels, on_device(): pl.pallas_call(load_kernel, out_shape=(jax.ShapeDtypeStruct((levs, lats +...  1.02 us
    ppermute x7, waiting for transfers between devices, send(): return lax.ppermute(x, ('lon', 'lat', 'lev'), pairs)  0.51 us
    pallas_call x1, Pallas kernels, on_device(): pl.pallas_call(lat_kernel, out_shape=(jax.ShapeDtypeStruct((levs, ext_til...  0.45 us
  transfers between devices with their start and end apart: 7, of which 1 were waited for; matrix products, arithmetic and copies ran while one was open for 0% of the time, Pallas kernels for 26%

profile of v3, /device:TPU:1, one launch (start us, length us, event | category | flops | bytes accessed | tf_op | source)
XLA Modules:
  0.0 18.8 jit_solution(13804454081470179835)
XLA Ops:
  0.0 0.0 copy-start.1
  0.0 0.0 copy-start
  0.0 1.0 %load.1 = (f32[4,5,8,256]{3,2,1,0:T(8,128)S(1)}, bf16[4,4,8,256]{3,2,1,0:T(8,128)(2,1)S(1)}, bf16[4,4,8,256]{3,2,1,0:T(8,128)(2,1)S(1)}, s32[64]{0:T(128)S(1)}, s32[64]{0:T(128)S(1)}, /*index=5*/s32[64]{0:T(128)S(1)}) custom-call(f32[8,4,4,256]{3,2,1,0:T(4,128)} %adj.1, f32[4,4,256]{2,1,0:T(4,128)} %wind_u.1, f32[4,4,256]{2,1,0:T(4,128)} %wind_w.1, ...), custom_call_target="tpu_custom_call" | custom-call | flops 1 | bytes 67108864 | tf_op jit(solution)/shard_map/load/pallas_call | solution.py:408
  1.0 2.2 %collective-permute-start = (bf16[4,4,8,256]{3,2,1,0:T(8,128)(2,1)S(1)}, bf16[4,4,8,256]{3,2,1,0:T(8,128)(2,1)S(1)}, u32[]{:S(2)}, u32[]{:S(2)}) collective-permute-start(bf16[4,4,8,256]{3,2,1,0:T(8,128)(2,1)S(1)} %get-tuple-element.22), channel_id=1, source_target_pairs={{0,4},{1,5},{2,6},{3,7},{4,0},{5,1},{6,2},{7,3},{8,12},{9,13},{10,... | collective-permute-start | bytes 196616 | tf_op jit(solution)/shard_map/ppermute | solution.py:48
  3.2 1.0 %collective-permute-start.1 = (bf16[4,4,8,256]{3,2,1,0:T(8,128)(2,1)S(1)}, bf16[4,4,8,256]{3,2,1,0:T(8,128)(2,1)S(1)}, u32[]{:S(2)}, u32[]{:S(2)}) collective-permute-start(bf16[4,4,8,256]{3,2,1,0:T(8,128)(2,1)S(1)} %get-tuple-element.23), channel_id=1, source_target_pairs={{0,1},{1,0},{2,3},{3,2},{4,8},{5,9},{6,10},{7,11},{8,4},{9,5},{10,... | collective-permute-start | bytes 196616 | tf_op jit(solution)/shard_map/ppermute | solution.py:48
  4.2 3.5 %obs.1 = (f32[4,4,8,256]{3,2,1,0:T(8,128)S(1)}, bf16[4,4,8,256]{3,2,1,0:T(8,128)(2,1)S(1)}) custom-call(s32[64]{0:T(128)S(1)} %get-tuple-element.24.owner, s32[64]{0:T(128)S(1)} %get-tuple-element.25.block_row, s32[64]{0:T(128)S(1)} %get-tuple-element.26.count, bf16[2048,128]{1,0:T(8,128)(2,1)} %bitcast.2, bf16[64,128,256]{2,1,0:T(8,128)(2,1)} %oper.1), custom_call_target="tpu_custom_call" | custom-call | flops 134217728 | bytes 12582912 | tf_op jit(solution)/shard_map/obs/pallas_call | solution.py:439
  7.7 0.0 collective-permute-done.from_a
  7.7 0.0 collective-permute-done.1.from_b
  7.7 0.4 %extend_lat.1 = (f32[4,13,8,256]{3,2,1,0:T(8,128)S(1)}, bf16[22,8,256]{2,1,0:T(8,128)(2,1)S(1)}, bf16[22,8,256]{2,1,0:T(8,128)(2,1)S(1)}, bf16[39,8,128]{2,1,0:T...) custom-call(f32[4,5,8,256]{3,2,1,0:T(8,128)S(1)} %get-tuple-element.21.own, ...), custom_call_target="tpu_custom_call" | custom-call | flops 1 | bytes 1048576 | tf_op jit(solution)/shard_map/extend_lat/pallas_call | solution.py:466
  8.1 0.0 collective-permute-start.2
  8.2 1.6 %collective-permute-start.3 = (bf16[22,8,256]{2,1,0:T(8,128)(2,1)S(1)}, bf16[22,8,256]{2,1,0:T(8,128)(2,1)S(1)}, u32[]{:S(2)}, u32[]{:S(2)}) collective-permute-start(bf16[22,8,256]{2,1,0:T(8,128)(2,1)S(1)} %get-tuple-element.30), channel_id=1, source_target_pairs={{0,4},{1,2},{2,1},{3,7},{4,0},{5,6},{6,5},{7,3},{8,12},{9,10},{10,... | collective-permute-start | bytes 270344 | tf_op jit(solution)/shard_map/ppermute | solution.py:48
  9.8 1.2 %collective-permute-start.4 = (bf16[39,8,128]{2,1,0:T(8,128)(2,1)S(1)}, bf16[39,8,128]{2,1,0:T(8,128)(2,1)S(1)}, u32[]{:S(2)}, u32[]{:S(2)}) collective-permute-start(bf16[39,8,128]{2,1,0:T(8,128)(2,1)S(1)} %get-tuple-element.34), channel_id=1, source_target_pairs={{0,16},{1,17},{2,18},{3,19},{4,20},{5,21},{6,22},{7,23},{8,24},{9,... | collective-permute-start | bytes 239624 | tf_op jit(solution)/shard_map/ppermute | solution.py:48
  11.0 2.0 %collective-permute-start.5 = (bf16[3,8,128]{2,1,0:T(8,128)(2,1)S(1)}, bf16[3,8,128]{2,1,0:T(8,128)(2,1)S(1)}, u32[]{:S(2)}, u32[]{:S(2)}) collective-permute-start(bf16[3,8,128]{2,1,0:T(8,128)(2,1)S(1)} %get-tuple-element.35), channel_id=1, source_target_pairs={{0,17},{1,16},{2,19},{3,18},{4,21},{5,20},{6,23},{7,22},{8,25},{9,... | collective-permute-start | bytes 18440 | tf_op jit(solution)/shard_map/ppermute | solution.py:48
  13.0 1.9 %collective-permute-start.6 = (bf16[3,8,128]{2,1,0:T(8,128)(2,1)S(1)}, bf16[3,8,128]{2,1,0:T(8,128)(2,1)S(1)}, u32[]{:S(2)}, u32[]{:S(2)}) collective-permute-start(bf16[3,8,128]{2,1,0:T(8,128)(2,1)S(1)} %get-tuple-element.36), channel_id=1, source_target_pairs={{0,16},{1,18},{2,17},{3,19},{4,20},{5,22},{6,21},{7,23},{8,24},{9,... | collective-permute-start | bytes 18440 | tf_op jit(solution)/shard_map/ppermute | solution.py:48
  15.0 0.0 collective-permute-done.2.from_a
  15.0 0.0 collective-permute-done.3.from_b
  15.0 0.0 copy-done.1
  15.0 0.0 copy-done
  15.0 1.5 %sub_steps.1 = (f32[4,4,8,256]{3,2,1,0:T(8,128)S(1)}, f32[96,8,128]{2,1,0:T(8,128)S(1)}) custom-call(f32[8]{0:T(128)S(1)} %copy-done, f32[16]{0:T(128)S(1)} %copy-done.1, f32[4,13,8,256]{3,2,1,0:T(8,128)S(1)} %get-tuple-element.28.ext, bf16[22,8,256]{2,1,0:T(8,128)(2,1)S(1)} %collective-permute-done.2.from_a, ...), custom_call_target="tpu_custom_call" | custom-call | flops 1 | bytes 8388608 | tf_op jit(solution)/shard_map/sub_steps/pallas_call | solution.py:499
  16.5 0.0 collective-permute-done.5.refs_1_
  16.5 0.5 %collective-permute-done.6.refs_2_ = bf16[3,8,128]{2,1,0:T(8,128)(2,1)S(1)} collective-permute-done((bf16[3,8,128]{2,1,0:T(8,128)(2,1)S(1)}, bf16[3,8,128]{2,1,0:T(8,128)(2,1)S(1)}, u32[]{:S(2)}, u32[]{:S(2)}) %collective-permute-start.6) | collective-permute-done | bytes 6176 | tf_op jit(solution)/shard_map/ppermute | solution.py:48
  17.0 0.0 collective-permute-done.4.refs_0_
  17.0 1.8 %edges.1 = f32[8,4,4,256]{3,2,1,0:T(4,128)} custom-call(f32[8]{0:T(128)S(1)} %copy-done, f32[16]{0:T(128)S(1)} %copy-done.1, f32[4,4,8,256]{3,2,1,0:T(8,128)S(1)} %get-tuple-element.31.main, f32[96,8,128]{2,1,0:T(8,128)S(1)} %get-tuple-element.32.own_rows, f32[4,4,8,256]{3,2,1,0:T(8,128)S(1)} %get-tuple-element.33.obs, ...), custom_call_target="tpu_custom_call" | custom-call | flops 1 | bytes 1048576 | tf_op jit(solution)/shard_map/edges/pallas_call | solution.py:513
Async XLA Ops:
  0.0 15.0 %copy-start.1 = (f32[16]{0:T(128)S(1)}, f32[16]{0:T(128)}, u32[]{:S(2)}) copy-start(f32[16]{0:T(128)} %vert.3) | copy-start | bytes 196
  0.0 15.0 %copy-start = (f32[8]{0:T(128)S(1)}, f32[8]{0:T(128)}, u32[]{:S(2)}) copy-start(f32[8]{0:T(128)} %diff.3) | copy-start | bytes 100
  1.0 6.6 %collective-permute-start = (bf16[4,4,8,256]{3,2,1,0:T(8,128)(2,1)S(1)}, bf16[4,4,8,256]{3,2,1,0:T(8,128)(2,1)S(1)}, u32[]{:S(2)}, u32[]{:S(2)}) collective-permute-start(bf16[4,4,8,256]{3,2,1,0:T(8,128)(2,1)S(1)} %get-tuple-element.22), channel_id=1, source_target_pairs={{0,4},{1,5},{2,6},{3,7},{4,0},{5,1},{6,2},{7,3},{8,12},{9,13},{10,... | collective-permute-start | bytes 196616 | tf_op jit(solution)/shard_map/ppermute | solution.py:48
  3.2 4.5 %collective-permute-start.1 = (bf16[4,4,8,256]{3,2,1,0:T(8,128)(2,1)S(1)}, bf16[4,4,8,256]{3,2,1,0:T(8,128)(2,1)S(1)}, u32[]{:S(2)}, u32[]{:S(2)}) collective-permute-start(bf16[4,4,8,256]{3,2,1,0:T(8,128)(2,1)S(1)} %get-tuple-element.23), channel_id=1, source_target_pairs={{0,1},{1,0},{2,3},{3,2},{4,8},{5,9},{6,10},{7,11},{8,4},{9,5},{10,... | collective-permute-start | bytes 196616 | tf_op jit(solution)/shard_map/ppermute | solution.py:48
  8.1 6.8 %collective-permute-start.2 = (bf16[22,8,256]{2,1,0:T(8,128)(2,1)S(1)}, bf16[22,8,256]{2,1,0:T(8,128)(2,1)S(1)}, u32[]{:S(2)}, u32[]{:S(2)}) collective-permute-start(bf16[22,8,256]{2,1,0:T(8,128)(2,1)S(1)} %get-tuple-element.29), channel_id=1, source_target_pairs={{0,1},{1,0},{2,3},{3,2},{4,5},{5,4},{6,7},{7,6},{8,9},{9,8},{10,11... | collective-permute-start | bytes 270344 | tf_op jit(solution)/shard_map/ppermute | solution.py:48
  8.2 6.8 %collective-permute-start.3 = (bf16[22,8,256]{2,1,0:T(8,128)(2,1)S(1)}, bf16[22,8,256]{2,1,0:T(8,128)(2,1)S(1)}, u32[]{:S(2)}, u32[]{:S(2)}) collective-permute-start(bf16[22,8,256]{2,1,0:T(8,128)(2,1)S(1)} %get-tuple-element.30), channel_id=1, source_target_pairs={{0,4},{1,2},{2,1},{3,7},{4,0},{5,6},{6,5},{7,3},{8,12},{9,10},{10,... | collective-permute-start | bytes 270344 | tf_op jit(solution)/shard_map/ppermute | solution.py:48
  9.8 7.2 %collective-permute-start.4 = (bf16[39,8,128]{2,1,0:T(8,128)(2,1)S(1)}, bf16[39,8,128]{2,1,0:T(8,128)(2,1)S(1)}, u32[]{:S(2)}, u32[]{:S(2)}) collective-permute-start(bf16[39,8,128]{2,1,0:T(8,128)(2,1)S(1)} %get-tuple-element.34), channel_id=1, source_target_pairs={{0,16},{1,17},{2,18},{3,19},{4,20},{5,21},{6,22},{7,23},{8,24},{9,... | collective-permute-start | bytes 239624 | tf_op jit(solution)/shard_map/ppermute | solution.py:48
  11.0 5.5 %collective-permute-start.5 = (bf16[3,8,128]{2,1,0:T(8,128)(2,1)S(1)}, bf16[3,8,128]{2,1,0:T(8,128)(2,1)S(1)}, u32[]{:S(2)}, u32[]{:S(2)}) collective-permute-start(bf16[3,8,128]{2,1,0:T(8,128)(2,1)S(1)} %get-tuple-element.35), channel_id=1, source_target_pairs={{0,17},{1,16},{2,19},{3,18},{4,21},{5,20},{6,23},{7,22},{8,25},{9,... | collective-permute-start | bytes 18440 | tf_op jit(solution)/shard_map/ppermute | solution.py:48
  13.0 4.0 %collective-permute-start.6 = (bf16[3,8,128]{2,1,0:T(8,128)(2,1)S(1)}, bf16[3,8,128]{2,1,0:T(8,128)(2,1)S(1)}, u32[]{:S(2)}, u32[]{:S(2)}) collective-permute-start(bf16[3,8,128]{2,1,0:T(8,128)(2,1)S(1)} %get-tuple-element.36), channel_id=1, source_target_pairs={{0,16},{1,18},{2,17},{3,19},{4,20},{5,22},{6,21},{7,23},{8,24},{9,... | collective-permute-start | bytes 18440 | tf_op jit(solution)/shard_map/ppermute | solution.py:48

commit v4 on v3

--- a/solution.py
+++ b/solution.py
@@ -11,6 +11,9 @@
 LANES = 128
 GROUP = 16
 PER_TILE = LANES // GROUP
+BITS = 4
+PIECE = 1 << BITS
+SHARES = (1,) * 3
 VMEM = pl.BlockSpec(memory_space=pltpu.VMEM)
 SMEM = pl.BlockSpec(memory_space=pltpu.SMEM)
 ANY = pl.BlockSpec(memory_space=pl.ANY)
@@ -91,34 +94,50 @@
             out[lev, STEPS] = own[lev, lats].astype(jnp.bfloat16)
 
 
-def obs_kernel(lats, owner, block_row, count, innov, oper, *refs):
+def chunks_of(blocks):
+    sizes, left = [], blocks
+    for share in SHARES:
+        sizes.append(min(left, max(1, blocks * share // sum(SHARES))))
+        left -= sizes[-1]
+    sizes[-1] += left
+    return [(sum(sizes[:n]), size) for n, size in enumerate(sizes) if size]
+
+
+def obs_kernel(lats, chunks, owner, block_row, count, innov, oper, *refs):
     outs, (lhs, rhs, acc, sem) = refs[:-4], refs[-4:]
-    blocks = oper.shape[0]
+    obs_rows = innov.shape[1]
+    blocks = oper.shape[0] // obs_rows
     rows = innov.shape[0] // blocks
     fields = 2 * lats
     levs = rows // fields
-    chunks = sem.shape[1]
-    per = blocks // chunks
-    copies = []
-    for n in range(chunks):
-        some, some_rows = pl.ds(n * per, per), pl.ds(n * per * rows, per * rows)
-        copies.append(
-            (
-                pltpu.make_async_copy(innov.at[some_rows], lhs.at[some_rows], sem.at[0, n]),
-                pltpu.make_async_copy(oper.at[some], rhs.at[some], sem.at[1, n]),
-            )
+    def fetch_oper(first, length, n):
+        some = pl.ds(pl.multiple_of(first, PIECE), pl.multiple_of(length, PIECE))
+        return pltpu.make_async_copy(oper.at[some], rhs.at[some], sem.at[1, n])
+
+    waits = {}
+    for n, (at, size) in enumerate(chunks):
+        some = pl.ds(at * rows, size * rows)
+        copy = pltpu.make_async_copy(innov.at[some], lhs.at[some], sem.at[0, n])
+        copy.start()
+        total = 0
+        for block in range(at, at + size):
+            length = lax.shift_right_logical(count[block] + (PIECE - 1), BITS)
+            length = lax.shift_left(length, BITS)
+            fetch_oper(block * obs_rows, length, n).start()
+            total = total + length
+        waits[at] = (copy, fetch_oper(0, total, n))
+    acc[...] = jnp.zeros_like(acc)
+    place = lax.broadcasted_iota(jnp.int32, (obs_rows, rhs.shape[1]), 0)
+    place = place.astype(jnp.float32).astype(jnp.bfloat16)
+    for block in range(blocks):
+        for copy in waits.get(block, ()):
+            copy.wait()
+        seen = place < count[block].astype(jnp.float32).astype(jnp.bfloat16)
+        masked = rhs[block * obs_rows : (block + 1) * obs_rows, :]
+        masked = jnp.where(seen, masked, jnp.zeros_like(masked))
+        product = jnp.dot(
+            lhs[block * rows : (block + 1) * rows, :], masked, preferred_element_type=jnp.float32
         )
-        for copy in copies[-1]:
-            copy.start()
-    acc[...] = jnp.zeros_like(acc)
-    lane = lax.broadcasted_iota(jnp.int32, (1, innov.shape[1]), 1)
-    for block in range(blocks):
-        if block % per == 0:
-            for copy in copies[block // per]:
-                copy.wait()
-        seen = (lane < count[block]).astype(jnp.float32).astype(jnp.bfloat16)
-        masked = lhs[block * rows : (block + 1) * rows, :] * seen
-        product = jnp.dot(masked, rhs[block], preferred_element_type=jnp.float32)
         spot = owner[block] * lats + block_row[block]
         product = product.astype(jnp.bfloat16).astype(jnp.float32)
         for half in range(acc.shape[1]):
@@ -424,9 +443,7 @@
     from_lat_a = send(to_lat_a, pair_up(sizes, 1, 0))
     from_lat_b = send(to_lat_b, pair_up(sizes, 1, 1))
 
-    chunks = 8
-    while blocks % chunks:
-        chunks //= 2
+    chunks = chunks_of(blocks)
     rows = fields * levs
     targets = n_lon * lats
     if n_lon == 2:
@@ -437,15 +454,15 @@
     else:
         obs_out = (jax.ShapeDtypeStruct((n_lon, levs, lats) + tile, f32),)
     obs = pl.pallas_call(
-        functools.partial(obs_kernel, lats),
+        functools.partial(obs_kernel, lats, chunks),
         out_shape=obs_out,
         in_specs=[SMEM] * 3 + [HBM] * 2,
         out_specs=(VMEM,) * len(obs_out),
         scratch_shapes=[
             pltpu.VMEM((blocks * rows, obs_rows), bf16),
-            pltpu.VMEM(obs_operator.shape, bf16),
+            pltpu.VMEM((blocks * obs_rows, lons), bf16),
             pltpu.VMEM((targets, lons // LANES, rows, LANES), f32),
-            pltpu.SemaphoreType.DMA((2, chunks)),
+            pltpu.SemaphoreType.DMA((2, len(chunks))),
         ],
         cost_estimate=cost(2 * blocks * rows * obs_rows * lons, 12 << 20),
         compiler_params=PARAMS,
@@ -455,7 +472,9 @@
         pltpu.with_memory_space_constraint(
             innovations.reshape(blocks * rows, obs_rows), pltpu.HBM
         ),
-        pltpu.with_memory_space_constraint(obs_operator, pltpu.HBM),
+        pltpu.with_memory_space_constraint(
+            obs_operator.reshape(blocks * obs_rows, lons), pltpu.HBM
+        ),
     )
 
     lev_tiles = sum(rows for _, _, rows in lev_rows(lats)) + 2 * (STEPS - 1)

time: 19 us -> 18.3 us (0.963)
  Pallas kernels: 8.23 us -> 7.53 us
    pallas_call x1, Pallas kernels: 3.49 us -> 2.8 us  [on_device(): pl.pallas_call(functools.partial(obs_kernel, lats, chunks), out_shape=obs...]
  transfers between devices with their start and end apart: 7 -> 7, of which waited for: 1 -> 1; matrix products, arithmetic and copies ran while one was open for 0% -> 0% of each run, Pallas kernels for 26% -> 24%
where the time goes in v4:
time: 18.3 us; the launch traced here: 18.1 us
  starting transfers between devices  9.99 us (55%)
  Pallas kernels  7.53 us (41%)
  waiting for transfers between devices  0.51 us (3%)
    ppermute x7, starting transfers between devices, send(): return lax.ppermute(x, ('lon', 'lat', 'lev'), pairs)  9.99 us
    pallas_call x1, Pallas kernels, on_device(): pl.pallas_call(functools.partial(obs_kernel, lats, chunks), out_shape=obs...  2.8 us
    pallas_call x1, Pallas kernels, on_device(): pl.pallas_call(functools.partial(edge_kernel, levs, lats, lev_tiles, len(...  1.78 us
    pallas_call x1, Pallas kernels, on_device(): pl.pallas_call(main_kernel, out_shape=(jax.ShapeDtypeStruct((levs, lats)...  1.48 us
    pallas_call x1, Pallas kernels, on_device(): pl.pallas_call(load_kernel, out_shape=(jax.ShapeDtypeStruct((levs, lats +...  1.02 us
    ppermute x7, waiting for transfers between devices, send(): return lax.ppermute(x, ('lon', 'lat', 'lev'), pairs)  0.51 us
    pallas_call x1, Pallas kernels, on_device(): pl.pallas_call(lat_kernel, out_shape=(jax.ShapeDtypeStruct((levs, ext_til...  0.45 us
  transfers between devices with their start and end apart: 7, of which 1 were waited for; matrix products, arithmetic and copies ran while one was open for 0% of the time, Pallas kernels for 24%

profile of v4, /device:TPU:1, one launch (start us, length us, event | category | flops | bytes accessed | tf_op | source)
XLA Modules:
  0.0 18.1 jit_solution(2625867351631273925)
XLA Ops:
  0.0 0.0 copy-start.1
  0.0 0.0 copy-start
  0.0 1.0 %load.1 = (f32[4,5,8,256]{3,2,1,0:T(8,128)S(1)}, bf16[4,4,8,256]{3,2,1,0:T(8,128)(2,1)S(1)}, bf16[4,4,8,256]{3,2,1,0:T(8,128)(2,1)S(1)}, s32[64]{0:T(128)S(1)}, s32[64]{0:T(128)S(1)}, /*index=5*/s32[64]{0:T(128)S(1)}) custom-call(f32[8,4,4,256]{3,2,1,0:T(4,128)} %adj.1, f32[4,4,256]{2,1,0:T(4,128)} %wind_u.1, f32[4,4,256]{2,1,0:T(4,128)} %wind_w.1, ...), custom_call_target="tpu_custom_call" | custom-call | flops 1 | bytes 67108864 | tf_op jit(solution)/shard_map/load/pallas_call | solution.py:427
  1.0 2.2 %collective-permute-start = (bf16[4,4,8,256]{3,2,1,0:T(8,128)(2,1)S(1)}, bf16[4,4,8,256]{3,2,1,0:T(8,128)(2,1)S(1)}, u32[]{:S(2)}, u32[]{:S(2)}) collective-permute-start(bf16[4,4,8,256]{3,2,1,0:T(8,128)(2,1)S(1)} %get-tuple-element.22), channel_id=1, source_target_pairs={{0,4},{1,5},{2,6},{3,7},{4,0},{5,1},{6,2},{7,3},{8,12},{9,13},{10,... | collective-permute-start | bytes 196616 | tf_op jit(solution)/shard_map/ppermute | solution.py:51
  3.2 1.0 %collective-permute-start.1 = (bf16[4,4,8,256]{3,2,1,0:T(8,128)(2,1)S(1)}, bf16[4,4,8,256]{3,2,1,0:T(8,128)(2,1)S(1)}, u32[]{:S(2)}, u32[]{:S(2)}) collective-permute-start(bf16[4,4,8,256]{3,2,1,0:T(8,128)(2,1)S(1)} %get-tuple-element.23), channel_id=1, source_target_pairs={{0,1},{1,0},{2,3},{3,2},{4,8},{5,9},{6,10},{7,11},{8,4},{9,5},{10,... | collective-permute-start | bytes 196616 | tf_op jit(solution)/shard_map/ppermute | solution.py:51
  4.2 2.8 %obs.1 = (f32[4,4,8,256]{3,2,1,0:T(8,128)S(1)}, bf16[4,4,8,256]{3,2,1,0:T(8,128)(2,1)S(1)}) custom-call(s32[64]{0:T(128)S(1)} %get-tuple-element.24.owner, s32[64]{0:T(128)S(1)} %get-tuple-element.25.block_row, s32[64]{0:T(128)S(1)} %get-tuple-element.26.count, bf16[2048,128]{1,0:T(8,128)(2,1)} %bitcast.4, bf16[8192,256]{1,0:T(8,128)(2,1)} %bitcast.3), custom_call_target="tpu_custom_call" | custom-call | flops 134217728 | bytes 12582912 | tf_op jit(solution)/shard_map/obs/pallas_call | solution.py:456
  7.0 0.0 collective-permute-done.from_a
  7.0 0.0 collective-permute-done.1.from_b
  7.0 0.4 %extend_lat.1 = (f32[4,13,8,256]{3,2,1,0:T(8,128)S(1)}, bf16[22,8,256]{2,1,0:T(8,128)(2,1)S(1)}, bf16[22,8,256]{2,1,0:T(8,128)(2,1)S(1)}, bf16[39,8,128]{2,1,0:T...) custom-call(f32[4,5,8,256]{3,2,1,0:T(8,128)S(1)} %get-tuple-element.21.own, ...), custom_call_target="tpu_custom_call" | custom-call | flops 1 | bytes 1048576 | tf_op jit(solution)/shard_map/extend_lat/pallas_call | solution.py:485
  7.4 0.0 collective-permute-start.2
  7.5 1.6 %collective-permute-start.3 = (bf16[22,8,256]{2,1,0:T(8,128)(2,1)S(1)}, bf16[22,8,256]{2,1,0:T(8,128)(2,1)S(1)}, u32[]{:S(2)}, u32[]{:S(2)}) collective-permute-start(bf16[22,8,256]{2,1,0:T(8,128)(2,1)S(1)} %get-tuple-element.30), channel_id=1, source_target_pairs={{0,4},{1,2},{2,1},{3,7},{4,0},{5,6},{6,5},{7,3},{8,12},{9,10},{10,... | collective-permute-start | bytes 270344 | tf_op jit(solution)/shard_map/ppermute | solution.py:51
  9.1 1.2 %collective-permute-start.4 = (bf16[39,8,128]{2,1,0:T(8,128)(2,1)S(1)}, bf16[39,8,128]{2,1,0:T(8,128)(2,1)S(1)}, u32[]{:S(2)}, u32[]{:S(2)}) collective-permute-start(bf16[39,8,128]{2,1,0:T(8,128)(2,1)S(1)} %get-tuple-element.34), channel_id=1, source_target_pairs={{0,16},{1,17},{2,18},{3,19},{4,20},{5,21},{6,22},{7,23},{8,24},{9,... | collective-permute-start | bytes 239624 | tf_op jit(solution)/shard_map/ppermute | solution.py:51
  10.3 2.0 %collective-permute-start.5 = (bf16[3,8,128]{2,1,0:T(8,128)(2,1)S(1)}, bf16[3,8,128]{2,1,0:T(8,128)(2,1)S(1)}, u32[]{:S(2)}, u32[]{:S(2)}) collective-permute-start(bf16[3,8,128]{2,1,0:T(8,128)(2,1)S(1)} %get-tuple-element.35), channel_id=1, source_target_pairs={{0,17},{1,16},{2,19},{3,18},{4,21},{5,20},{6,23},{7,22},{8,25},{9,... | collective-permute-start | bytes 18440 | tf_op jit(solution)/shard_map/ppermute | solution.py:51
  12.4 1.9 %collective-permute-start.6 = (bf16[3,8,128]{2,1,0:T(8,128)(2,1)S(1)}, bf16[3,8,128]{2,1,0:T(8,128)(2,1)S(1)}, u32[]{:S(2)}, u32[]{:S(2)}) collective-permute-start(bf16[3,8,128]{2,1,0:T(8,128)(2,1)S(1)} %get-tuple-element.36), channel_id=1, source_target_pairs={{0,16},{1,18},{2,17},{3,19},{4,20},{5,22},{6,21},{7,23},{8,24},{9,... | collective-permute-start | bytes 18440 | tf_op jit(solution)/shard_map/ppermute | solution.py:51
  14.3 0.0 collective-permute-done.2.from_a
  14.3 0.0 collective-permute-done.3.from_b
  14.3 0.0 copy-done.1
  14.3 0.0 copy-done
  14.3 1.5 %sub_steps.1 = (f32[4,4,8,256]{3,2,1,0:T(8,128)S(1)}, f32[96,8,128]{2,1,0:T(8,128)S(1)}) custom-call(f32[8]{0:T(128)S(1)} %copy-done, f32[16]{0:T(128)S(1)} %copy-done.1, f32[4,13,8,256]{3,2,1,0:T(8,128)S(1)} %get-tuple-element.28.ext, bf16[22,8,256]{2,1,0:T(8,128)(2,1)S(1)} %collective-permute-done.2.from_a, ...), custom_call_target="tpu_custom_call" | custom-call | flops 1 | bytes 8388608 | tf_op jit(solution)/shard_map/sub_steps/pallas_call | solution.py:518
  15.8 0.0 collective-permute-done.5.refs_1_
  15.8 0.5 %collective-permute-done.6.refs_2_ = bf16[3,8,128]{2,1,0:T(8,128)(2,1)S(1)} collective-permute-done((bf16[3,8,128]{2,1,0:T(8,128)(2,1)S(1)}, bf16[3,8,128]{2,1,0:T(8,128)(2,1)S(1)}, u32[]{:S(2)}, u32[]{:S(2)}) %collective-permute-start.6) | collective-permute-done | bytes 6176 | tf_op jit(solution)/shard_map/ppermute | solution.py:51
  16.3 0.0 collective-permute-done.4.refs_0_
  16.3 1.8 %edges.1 = f32[8,4,4,256]{3,2,1,0:T(4,128)} custom-call(f32[8]{0:T(128)S(1)} %copy-done, f32[16]{0:T(128)S(1)} %copy-done.1, f32[4,4,8,256]{3,2,1,0:T(8,128)S(1)} %get-tuple-element.31.main, f32[96,8,128]{2,1,0:T(8,128)S(1)} %get-tuple-element.32.own_rows, f32[4,4,8,256]{3,2,1,0:T(8,128)S(1)} %get-tuple-element.33.obs, ...), custom_call_target="tpu_custom_call" | custom-call | flops 1 | bytes 1048576 | tf_op jit(solution)/shard_map/edges/pallas_call | solution.py:532
Async XLA Ops:
  0.0 14.3 %copy-start.1 = (f32[16]{0:T(128)S(1)}, f32[16]{0:T(128)}, u32[]{:S(2)}) copy-start(f32[16]{0:T(128)} %vert.3) | copy-start | bytes 196
  0.0 14.3 %copy-start = (f32[8]{0:T(128)S(1)}, f32[8]{0:T(128)}, u32[]{:S(2)}) copy-start(f32[8]{0:T(128)} %diff.3) | copy-start | bytes 100
  1.0 5.9 %collective-permute-start = (bf16[4,4,8,256]{3,2,1,0:T(8,128)(2,1)S(1)}, bf16[4,4,8,256]{3,2,1,0:T(8,128)(2,1)S(1)}, u32[]{:S(2)}, u32[]{:S(2)}) collective-permute-start(bf16[4,4,8,256]{3,2,1,0:T(8,128)(2,1)S(1)} %get-tuple-element.22), channel_id=1, source_target_pairs={{0,4},{1,5},{2,6},{3,7},{4,0},{5,1},{6,2},{7,3},{8,12},{9,13},{10,... | collective-permute-start | bytes 196616 | tf_op jit(solution)/shard_map/ppermute | solution.py:51
  3.2 3.8 %collective-permute-start.1 = (bf16[4,4,8,256]{3,2,1,0:T(8,128)(2,1)S(1)}, bf16[4,4,8,256]{3,2,1,0:T(8,128)(2,1)S(1)}, u32[]{:S(2)}, u32[]{:S(2)}) collective-permute-start(bf16[4,4,8,256]{3,2,1,0:T(8,128)(2,1)S(1)} %get-tuple-element.23), channel_id=1, source_target_pairs={{0,1},{1,0},{2,3},{3,2},{4,8},{5,9},{6,10},{7,11},{8,4},{9,5},{10,... | collective-permute-start | bytes 196616 | tf_op jit(solution)/shard_map/ppermute | solution.py:51
  7.4 6.9 %collective-permute-start.2 = (bf16[22,8,256]{2,1,0:T(8,128)(2,1)S(1)}, bf16[22,8,256]{2,1,0:T(8,128)(2,1)S(1)}, u32[]{:S(2)}, u32[]{:S(2)}) collective-permute-start(bf16[22,8,256]{2,1,0:T(8,128)(2,1)S(1)} %get-tuple-element.29), channel_id=1, source_target_pairs={{0,1},{1,0},{2,3},{3,2},{4,5},{5,4},{6,7},{7,6},{8,9},{9,8},{10,11... | collective-permute-start | bytes 270344 | tf_op jit(solution)/shard_map/ppermute | solution.py:51
  7.5 6.8 %collective-permute-start.3 = (bf16[22,8,256]{2,1,0:T(8,128)(2,1)S(1)}, bf16[22,8,256]{2,1,0:T(8,128)(2,1)S(1)}, u32[]{:S(2)}, u32[]{:S(2)}) collective-permute-start(bf16[22,8,256]{2,1,0:T(8,128)(2,1)S(1)} %get-tuple-element.30), channel_id=1, source_target_pairs={{0,4},{1,2},{2,1},{3,7},{4,0},{5,6},{6,5},{7,3},{8,12},{9,10},{10,... | collective-permute-start | bytes 270344 | tf_op jit(solution)/shard_map/ppermute | solution.py:51
  9.1 7.2 %collective-permute-start.4 = (bf16[39,8,128]{2,1,0:T(8,128)(2,1)S(1)}, bf16[39,8,128]{2,1,0:T(8,128)(2,1)S(1)}, u32[]{:S(2)}, u32[]{:S(2)}) collective-permute-start(bf16[39,8,128]{2,1,0:T(8,128)(2,1)S(1)} %get-tuple-element.34), channel_id=1, source_target_pairs={{0,16},{1,17},{2,18},{3,19},{4,20},{5,21},{6,22},{7,23},{8,24},{9,... | collective-permute-start | bytes 239624 | tf_op jit(solution)/shard_map/ppermute | solution.py:51
  10.3 5.5 %collective-permute-start.5 = (bf16[3,8,128]{2,1,0:T(8,128)(2,1)S(1)}, bf16[3,8,128]{2,1,0:T(8,128)(2,1)S(1)}, u32[]{:S(2)}, u32[]{:S(2)}) collective-permute-start(bf16[3,8,128]{2,1,0:T(8,128)(2,1)S(1)} %get-tuple-element.35), channel_id=1, source_target_pairs={{0,17},{1,16},{2,19},{3,18},{4,21},{5,20},{6,23},{7,22},{8,25},{9,... | collective-permute-start | bytes 18440 | tf_op jit(solution)/shard_map/ppermute | solution.py:51
  12.4 4.0 %collective-permute-start.6 = (bf16[3,8,128]{2,1,0:T(8,128)(2,1)S(1)}, bf16[3,8,128]{2,1,0:T(8,128)(2,1)S(1)}, u32[]{:S(2)}, u32[]{:S(2)}) collective-permute-start(bf16[3,8,128]{2,1,0:T(8,128)(2,1)S(1)} %get-tuple-element.36), channel_id=1, source_target_pairs={{0,16},{1,18},{2,17},{3,19},{4,20},{5,22},{6,21},{7,23},{8,24},{9,... | collective-permute-start | bytes 18440 | tf_op jit(solution)/shard_map/ppermute | solution.py:51

commit v5 on v4

--- a/solution.py
+++ b/solution.py
@@ -6,6 +6,7 @@
 from jax.experimental import pallas as pl
 from jax.experimental.pallas import tpu as pltpu
 from jax.sharding import PartitionSpec as P
+
 
 STEPS = 3
 LANES = 128
@@ -110,6 +111,7 @@
     rows = innov.shape[0] // blocks
     fields = 2 * lats
     levs = rows // fields
+
     def fetch_oper(first, length, n):
         some = pl.ds(pl.multiple_of(first, PIECE), pl.multiple_of(length, PIECE))
         return pltpu.make_async_copy(oper.at[some], rhs.at[some], sem.at[1, n])
@@ -391,14 +393,19 @@
                 value = jnp.where(lane < STEPS, first, value)
             if part == parts - 1:
                 value = jnp.where(lane >= LANES - STEPS, last, value)
-            result[k, j, :, part * LANES : (part + 1) * LANES] = value + total(k, j, part)
+            result[part, pl.ds(k * lats + j, fields, stride=levs * lats), :] = value + total(
+                k, j, part
+            )
 
     steps.run(diff, vert, (fields, LANES), first_rows, wind, (rows_a, rows_b), emit)
-    copies = [
-        pltpu.make_async_copy(result.at[:, :, f, :], out.at[f], sem.at[f]) for f in range(fields)
-    ]
-    for copy in copies:
-        copy.start()
+    copies = []
+    for part in range(parts):
+        some = pl.ds(part * LANES, LANES)
+        source = result.at[part].reshape(fields, levs, lats, LANES)
+        copies.append(
+            pltpu.make_async_copy(source, out.at[:, :, :, some], sem.at[part])
+        )
+        copies[-1].start()
     for copy in copies:
         copy.wait()
 
@@ -538,7 +545,7 @@
             pltpu.VMEM(edge_shape, f32),
             pltpu.VMEM((grid_rows, fields, LANES), f32),
             pltpu.VMEM((grid_rows, fields, LANES), f32),
-            pltpu.VMEM((levs, lats) + tile, f32),
+            pltpu.VMEM((lons // LANES, fields * levs * lats, LANES), f32),
             pltpu.SemaphoreType.DMA((fields,)),
         ],
         cost_estimate=cost(1, 1 << 20),
@@ -561,6 +568,7 @@
         P(("lon", "lat")),
     )
     out_specs = P(None, "lev", "lat", "lon")
+
     return jax.shard_map(
         on_device, mesh=mesh, in_specs=in_specs, out_specs=out_specs, check_vma=False
     )

time: 18.3 us -> 18.3 us (level)
  no operation moved by 1% of the time
where the time goes in v5:
time: 18.3 us; the launch traced here: 18.1 us
  starting transfers between devices  10 us (55%)
  Pallas kernels  7.57 us (41%)
  waiting for transfers between devices  0.46 us (3%)
    ppermute x7, starting transfers between devices, send(): return lax.ppermute(x, ('lon', 'lat', 'lev'), pairs)  10 us
    pallas_call x1, Pallas kernels, on_device(): pl.pallas_call(functools.partial(obs_kernel, lats, chunks), out_shape=obs...  2.82 us
    pallas_call x1, Pallas kernels, on_device(): pl.pallas_call(functools.partial(edge_kernel, levs, lats, lev_tiles, len(...  1.8 us
    pallas_call x1, Pallas kernels, on_device(): pl.pallas_call(main_kernel, out_shape=(jax.ShapeDtypeStruct((levs, lats)...  1.48 us
    pallas_call x1, Pallas kernels, on_device(): pl.pallas_call(load_kernel, out_shape=(jax.ShapeDtypeStruct((levs, lats +...  1.02 us
    ppermute x7, waiting for transfers between devices, send(): return lax.ppermute(x, ('lon', 'lat', 'lev'), pairs)  0.46 us
    pallas_call x1, Pallas kernels, on_device(): pl.pallas_call(lat_kernel, out_shape=(jax.ShapeDtypeStruct((levs, ext_til...  0.45 us
  transfers between devices with their start and end apart: 7, of which 1 were waited for; matrix products, arithmetic and copies ran while one was open for 0% of the time, Pallas kernels for 24%

profile of v5, /device:TPU:1, one launch (start us, length us, event | category | flops | bytes accessed | tf_op | source)
XLA Modules:
  0.0 18.1 jit_solution(7239063272578229811)
XLA Ops:
  0.0 0.0 copy-start.1
  0.0 0.0 copy-start
  0.0 1.0 %load.1 = (f32[4,5,8,256]{3,2,1,0:T(8,128)S(1)}, bf16[4,4,8,256]{3,2,1,0:T(8,128)(2,1)S(1)}, bf16[4,4,8,256]{3,2,1,0:T(8,128)(2,1)S(1)}, s32[64]{0:T(128)S(1)}, s32[64]{0:T(128)S(1)}, /*index=5*/s32[64]{0:T(128)S(1)}) custom-call(f32[8,4,4,256]{3,2,1,0:T(4,128)} %adj.1, f32[4,4,256]{2,1,0:T(4,128)} %wind_u.1, f32[4,4,256]{2,1,0:T(4,128)} %wind_w.1, ...), custom_call_target="tpu_custom_call" | custom-call | flops 1 | bytes 67108864 | tf_op jit(solution)/shard_map/load/pallas_call | solution.py:434
  1.0 2.2 %collective-permute-start = (bf16[4,4,8,256]{3,2,1,0:T(8,128)(2,1)S(1)}, bf16[4,4,8,256]{3,2,1,0:T(8,128)(2,1)S(1)}, u32[]{:S(2)}, u32[]{:S(2)}) collective-permute-start(bf16[4,4,8,256]{3,2,1,0:T(8,128)(2,1)S(1)} %get-tuple-element.22), channel_id=1, source_target_pairs={{0,4},{1,5},{2,6},{3,7},{4,0},{5,1},{6,2},{7,3},{8,12},{9,13},{10,... | collective-permute-start | bytes 196616 | tf_op jit(solution)/shard_map/ppermute | solution.py:52
  3.2 1.0 %collective-permute-start.1 = (bf16[4,4,8,256]{3,2,1,0:T(8,128)(2,1)S(1)}, bf16[4,4,8,256]{3,2,1,0:T(8,128)(2,1)S(1)}, u32[]{:S(2)}, u32[]{:S(2)}) collective-permute-start(bf16[4,4,8,256]{3,2,1,0:T(8,128)(2,1)S(1)} %get-tuple-element.23), channel_id=1, source_target_pairs={{0,1},{1,0},{2,3},{3,2},{4,8},{5,9},{6,10},{7,11},{8,4},{9,5},{10,... | collective-permute-start | bytes 196616 | tf_op jit(solution)/shard_map/ppermute | solution.py:52
  4.2 2.8 %obs.1 = (f32[4,4,8,256]{3,2,1,0:T(8,128)S(1)}, bf16[4,4,8,256]{3,2,1,0:T(8,128)(2,1)S(1)}) custom-call(s32[64]{0:T(128)S(1)} %get-tuple-element.24.owner, s32[64]{0:T(128)S(1)} %get-tuple-element.25.block_row, s32[64]{0:T(128)S(1)} %get-tuple-element.26.count, bf16[2048,128]{1,0:T(8,128)(2,1)} %bitcast.4, bf16[8192,256]{1,0:T(8,128)(2,1)} %bitcast.3), custom_call_target="tpu_custom_call" | custom-call | flops 134217728 | bytes 12582912 | tf_op jit(solution)/shard_map/obs/pallas_call | solution.py:463
  7.0 0.0 collective-permute-done.from_a
  7.0 0.0 collective-permute-done.1.from_b
  7.0 0.4 %extend_lat.1 = (f32[4,13,8,256]{3,2,1,0:T(8,128)S(1)}, bf16[22,8,256]{2,1,0:T(8,128)(2,1)S(1)}, bf16[22,8,256]{2,1,0:T(8,128)(2,1)S(1)}, bf16[39,8,128]{2,1,0:T...) custom-call(f32[4,5,8,256]{3,2,1,0:T(8,128)S(1)} %get-tuple-element.21.own, ...), custom_call_target="tpu_custom_call" | custom-call | flops 1 | bytes 1048576 | tf_op jit(solution)/shard_map/extend_lat/pallas_call | solution.py:492
  7.5 0.0 collective-permute-start.2
  7.5 1.6 %collective-permute-start.3 = (bf16[22,8,256]{2,1,0:T(8,128)(2,1)S(1)}, bf16[22,8,256]{2,1,0:T(8,128)(2,1)S(1)}, u32[]{:S(2)}, u32[]{:S(2)}) collective-permute-start(bf16[22,8,256]{2,1,0:T(8,128)(2,1)S(1)} %get-tuple-element.30), channel_id=1, source_target_pairs={{0,4},{1,2},{2,1},{3,7},{4,0},{5,6},{6,5},{7,3},{8,12},{9,10},{10,... | collective-permute-start | bytes 270344 | tf_op jit(solution)/shard_map/ppermute | solution.py:52
  9.1 1.2 %collective-permute-start.4 = (bf16[39,8,128]{2,1,0:T(8,128)(2,1)S(1)}, bf16[39,8,128]{2,1,0:T(8,128)(2,1)S(1)}, u32[]{:S(2)}, u32[]{:S(2)}) collective-permute-start(bf16[39,8,128]{2,1,0:T(8,128)(2,1)S(1)} %get-tuple-element.34), channel_id=1, source_target_pairs={{0,16},{1,17},{2,18},{3,19},{4,20},{5,21},{6,22},{7,23},{8,24},{9,... | collective-permute-start | bytes 239624 | tf_op jit(solution)/shard_map/ppermute | solution.py:52
  10.4 2.0 %collective-permute-start.5 = (bf16[3,8,128]{2,1,0:T(8,128)(2,1)S(1)}, bf16[3,8,128]{2,1,0:T(8,128)(2,1)S(1)}, u32[]{:S(2)}, u32[]{:S(2)}) collective-permute-start(bf16[3,8,128]{2,1,0:T(8,128)(2,1)S(1)} %get-tuple-element.35), channel_id=1, source_target_pairs={{0,17},{1,16},{2,19},{3,18},{4,21},{5,20},{6,23},{7,22},{8,25},{9,... | collective-permute-start | bytes 18440 | tf_op jit(solution)/shard_map/ppermute | solution.py:52
  12.4 2.0 %collective-permute-start.6 = (bf16[3,8,128]{2,1,0:T(8,128)(2,1)S(1)}, bf16[3,8,128]{2,1,0:T(8,128)(2,1)S(1)}, u32[]{:S(2)}, u32[]{:S(2)}) collective-permute-start(bf16[3,8,128]{2,1,0:T(8,128)(2,1)S(1)} %get-tuple-element.36), channel_id=1, source_target_pairs={{0,16},{1,18},{2,17},{3,19},{4,20},{5,22},{6,21},{7,23},{8,24},{9,... | collective-permute-start | bytes 18440 | tf_op jit(solution)/shard_map/ppermute | solution.py:52
  14.3 0.0 collective-permute-done.2.from_a
  14.4 0.0 collective-permute-done.3.from_b
  14.4 0.0 copy-done.1
  14.4 0.0 copy-done
  14.4 1.5 %sub_steps.1 = (f32[4,4,8,256]{3,2,1,0:T(8,128)S(1)}, f32[96,8,128]{2,1,0:T(8,128)S(1)}) custom-call(f32[8]{0:T(128)S(1)} %copy-done, f32[16]{0:T(128)S(1)} %copy-done.1, f32[4,13,8,256]{3,2,1,0:T(8,128)S(1)} %get-tuple-element.28.ext, bf16[22,8,256]{2,1,0:T(8,128)(2,1)S(1)} %collective-permute-done.2.from_a, ...), custom_call_target="tpu_custom_call" | custom-call | flops 1 | bytes 8388608 | tf_op jit(solution)/shard_map/sub_steps/pallas_call | solution.py:525
  15.9 0.0 collective-permute-done.5.refs_1_
  15.9 0.4 %collective-permute-done.6.refs_2_ = bf16[3,8,128]{2,1,0:T(8,128)(2,1)S(1)} collective-permute-done((bf16[3,8,128]{2,1,0:T(8,128)(2,1)S(1)}, bf16[3,8,128]{2,1,0:T(8,128)(2,1)S(1)}, u32[]{:S(2)}, u32[]{:S(2)}) %collective-permute-start.6) | collective-permute-done | bytes 6176 | tf_op jit(solution)/shard_map/ppermute | solution.py:52
  16.3 0.0 collective-permute-done.4.refs_0_
  16.3 1.8 %edges.1 = f32[8,4,4,256]{3,2,1,0:T(4,128)} custom-call(f32[8]{0:T(128)S(1)} %copy-done, f32[16]{0:T(128)S(1)} %copy-done.1, f32[4,4,8,256]{3,2,1,0:T(8,128)S(1)} %get-tuple-element.31.main, f32[96,8,128]{2,1,0:T(8,128)S(1)} %get-tuple-element.32.own_rows, f32[4,4,8,256]{3,2,1,0:T(8,128)S(1)} %get-tuple-element.33.obs, ...), custom_call_target="tpu_custom_call" | custom-call | flops 1 | bytes 1048576 | tf_op jit(solution)/shard_map/edges/pallas_call | solution.py:539
Async XLA Ops:
  0.0 14.4 %copy-start.1 = (f32[16]{0:T(128)S(1)}, f32[16]{0:T(128)}, u32[]{:S(2)}) copy-start(f32[16]{0:T(128)} %vert.3) | copy-start | bytes 196
  0.0 14.4 %copy-start = (f32[8]{0:T(128)S(1)}, f32[8]{0:T(128)}, u32[]{:S(2)}) copy-start(f32[8]{0:T(128)} %diff.3) | copy-start | bytes 100
  1.0 6.0 %collective-permute-start = (bf16[4,4,8,256]{3,2,1,0:T(8,128)(2,1)S(1)}, bf16[4,4,8,256]{3,2,1,0:T(8,128)(2,1)S(1)}, u32[]{:S(2)}, u32[]{:S(2)}) collective-permute-start(bf16[4,4,8,256]{3,2,1,0:T(8,128)(2,1)S(1)} %get-tuple-element.22), channel_id=1, source_target_pairs={{0,4},{1,5},{2,6},{3,7},{4,0},{5,1},{6,2},{7,3},{8,12},{9,13},{10,... | collective-permute-start | bytes 196616 | tf_op jit(solution)/shard_map/ppermute | solution.py:52
  3.2 3.8 %collective-permute-start.1 = (bf16[4,4,8,256]{3,2,1,0:T(8,128)(2,1)S(1)}, bf16[4,4,8,256]{3,2,1,0:T(8,128)(2,1)S(1)}, u32[]{:S(2)}, u32[]{:S(2)}) collective-permute-start(bf16[4,4,8,256]{3,2,1,0:T(8,128)(2,1)S(1)} %get-tuple-element.23), channel_id=1, source_target_pairs={{0,1},{1,0},{2,3},{3,2},{4,8},{5,9},{6,10},{7,11},{8,4},{9,5},{10,... | collective-permute-start | bytes 196616 | tf_op jit(solution)/shard_map/ppermute | solution.py:52
  7.5 6.9 %collective-permute-start.2 = (bf16[22,8,256]{2,1,0:T(8,128)(2,1)S(1)}, bf16[22,8,256]{2,1,0:T(8,128)(2,1)S(1)}, u32[]{:S(2)}, u32[]{:S(2)}) collective-permute-start(bf16[22,8,256]{2,1,0:T(8,128)(2,1)S(1)} %get-tuple-element.29), channel_id=1, source_target_pairs={{0,1},{1,0},{2,3},{3,2},{4,5},{5,4},{6,7},{7,6},{8,9},{9,8},{10,11... | collective-permute-start | bytes 270344 | tf_op jit(solution)/shard_map/ppermute | solution.py:52
  7.5 6.8 %collective-permute-start.3 = (bf16[22,8,256]{2,1,0:T(8,128)(2,1)S(1)}, bf16[22,8,256]{2,1,0:T(8,128)(2,1)S(1)}, u32[]{:S(2)}, u32[]{:S(2)}) collective-permute-start(bf16[22,8,256]{2,1,0:T(8,128)(2,1)S(1)} %get-tuple-element.30), channel_id=1, source_target_pairs={{0,4},{1,2},{2,1},{3,7},{4,0},{5,6},{6,5},{7,3},{8,12},{9,10},{10,... | collective-permute-start | bytes 270344 | tf_op jit(solution)/shard_map/ppermute | solution.py:52
  9.1 7.2 %collective-permute-start.4 = (bf16[39,8,128]{2,1,0:T(8,128)(2,1)S(1)}, bf16[39,8,128]{2,1,0:T(8,128)(2,1)S(1)}, u32[]{:S(2)}, u32[]{:S(2)}) collective-permute-start(bf16[39,8,128]{2,1,0:T(8,128)(2,1)S(1)} %get-tuple-element.34), channel_id=1, source_target_pairs={{0,16},{1,17},{2,18},{3,19},{4,20},{5,21},{6,22},{7,23},{8,24},{9,... | collective-permute-start | bytes 239624 | tf_op jit(solution)/shard_map/ppermute | solution.py:52
  10.4 5.5 %collective-permute-start.5 = (bf16[3,8,128]{2,1,0:T(8,128)(2,1)S(1)}, bf16[3,8,128]{2,1,0:T(8,128)(2,1)S(1)}, u32[]{:S(2)}, u32[]{:S(2)}) collective-permute-start(bf16[3,8,128]{2,1,0:T(8,128)(2,1)S(1)} %get-tuple-element.35), channel_id=1, source_target_pairs={{0,17},{1,16},{2,19},{3,18},{4,21},{5,20},{6,23},{7,22},{8,25},{9,... | collective-permute-start | bytes 18440 | tf_op jit(solution)/shard_map/ppermute | solution.py:52
  12.4 4.0 %collective-permute-start.6 = (bf16[3,8,128]{2,1,0:T(8,128)(2,1)S(1)}, bf16[3,8,128]{2,1,0:T(8,128)(2,1)S(1)}, u32[]{:S(2)}, u32[]{:S(2)}) collective-permute-start(bf16[3,8,128]{2,1,0:T(8,128)(2,1)S(1)} %get-tuple-element.36), channel_id=1, source_target_pairs={{0,16},{1,18},{2,17},{3,19},{4,20},{5,22},{6,21},{7,23},{8,24},{9,... | collective-permute-start | bytes 18440 | tf_op jit(solution)/shard_map/ppermute | solution.py:52
